TPU v7x, 1024 devices: a whole 4x4x32 slice. The times are simulated.
1024 devices in a mesh: elem: 128 (over x, z), span: 8 (over y, core).
Axes of the slice: x: 4, y: 4, z: 32, core: 2. Of those that a mesh axis runs over, the one named last changes fastest.
Arguments:
- adjoint: float32 [16384, 5, 512], P(('span', 'elem')), may hold values from -6 to 6
- density: float32 [16384], P(('span', 'elem')), may hold values from 0.5 to 2
- velocity: float32 [3, 16384], P(None, ('span', 'elem')), may hold values from -1.2 to 1.2
- pressure: float32 [16384], P(('span', 'elem')), may hold values from 0.4 to 1.6
- metric: float32 [3, 16384], P(None, ('span', 'elem')), may hold values from 0.5 to 2
- face_source: int32 [512, 4], P('elem'), may hold values from 0 to 23, as said below
- face_flip: int32 [512, 4], P('elem'), may hold values from 0 to 1, as said below
- face_tag: int32 [512, 4], P('elem'), may hold values from 0 to 2, as said below
- send_list: int32 [512, 2], P('elem'), may hold values from 0 to 15, as said below
Outputs:
- adjoint_next: float32 [16384, 5, 512], P(('span', 'elem'))
- register: float32 [16384, 5, 512], P(('span', 'elem'))
Inputs may be any that keep to these rules, and one draw needn't show every extreme that they name: `face_source`: On tagged faces the value is the face's own number 4 c + f. Some partition uses all 2 entries of its blocks to the partitions one and two after it in every draw. `face_flip`: equal on the two faces of an interior pair; 0 on tagged faces. `face_tag`: 0 interior, 1 slip wall, 2 far field; every partition has a tagged face. `send_list`: row 4 p + r lists faces of partition p, numbered 4 c + f; the first n of them, with 1 <= n <= 2, are the faces whose neighbours lie on partition p + (1, 2, -1, -2)[r], in the order in which that partition names them; the rest are named by no face.
All inputs are finite; a program needn't handle non-finite values.
Results may differ from a plain program's by a relative error of at most 0.000068.
Values sent between devices are 32-bit elements; how exact they have to be, the bound alone decides.
A program may use at most 32 MiB of HBM per device.

v0:
```python
import jax
import jax.numpy as jnp
import numpy as np
from jax import lax
from jax.sharding import PartitionSpec as P

gamma_gas = 1.4
lift_end = 28.0
time_step = 0.02
section_a2 = -567301805773.0 / 1357537059087.0
section_b1 = 1432997174477.0 / 9575080441755.0
section_b2 = 5161836677717.0 / 13612068292357.0


def passed_along(block, axis, distance):
    devices = range(lax.axis_size(axis))
    route = [((i - distance) % len(devices), i) for i in devices]
    return lax.ppermute(block, axis, route)


def lobatto_nodes():
    return [
        -1.0,
        -0.8717401485096066,
        -0.5917001814331423,
        -0.2092992179024789,
        0.2092992179024789,
        0.5917001814331423,
        0.8717401485096066,
        1.0,
    ]


def lobatto_derivative():
    positions = np.array(lobatto_nodes())
    total_nodes = positions.shape[0]
    differences = positions[:, None] - positions[None, :] + np.eye(total_nodes)
    weights = 1.0 / np.prod(differences, axis=1)
    matrix_out = weights[None, :] / weights[:, None] / differences
    matrix_out = matrix_out * (1.0 - np.eye(total_nodes))
    return matrix_out - np.eye(total_nodes) * np.sum(matrix_out, axis=1)[:, None]


def derivative_tables():
    matrix_in = lobatto_derivative()
    along_x = np.kron(np.eye(64), matrix_in)
    along_y = np.kron(np.eye(8), np.kron(matrix_in, np.eye(8)))
    along_z = np.kron(matrix_in, np.eye(64))
    return np.concatenate([along_x.T, along_y.T, along_z.T], axis=1)


def face_table():
    picker = np.zeros((512, 384))
    for outer_index in range(8):
        for inner_index in range(8):
            column = outer_index * 8 + inner_index
            nodes_list = [
                outer_index * 64 + inner_index * 8,
                outer_index * 64 + inner_index * 8 + 7,
                outer_index * 64 + inner_index,
                outer_index * 64 + 56 + inner_index,
                outer_index * 8 + inner_index,
                448 + outer_index * 8 + inner_index,
            ]
            for face_index in range(6):
                picker[nodes_list[face_index], 64 * face_index + column] = 1.0
    return picker


def mirror_table():
    mirror = np.zeros((320, 320))
    for position in range(320):
        mirror[position - position % 8 + 7 - position % 8, position] = 1.0
    return mirror


def wall_table(columns):
    signs = np.ones((4, 5, 64))
    for face_index in range(4):
        signs[face_index, 1 + face_index // 2, :] = -1.0
    return np.tile(signs.reshape(4, 320), (columns, 1))


def adjoint_flux(values, direction, density_c, along, stiffness):
    components = [along * values[..., component, :] for component in range(5)]
    components[1 + direction] = (
        components[1 + direction] + density_c * values[..., 0, :] + stiffness * values[..., 4, :]
    )
    components[4] = components[4] + values[..., 1 + direction, :] / density_c
    return jnp.stack(components, axis=-2)


def volume_terms(derivatives, density_c, velocity_c, pressure_c, metric_c):
    stiffness = gamma_gas * pressure_c
    terms_list = [
        metric_c[direction][..., None]
        * adjoint_flux(
            derivatives[direction], direction, density_c, velocity_c[direction], stiffness
        )
        for direction in range(3)
    ]
    return terms_list[0] + terms_list[1] + terms_list[2]


def face_terms(difference, density_c, velocity_c, pressure_c, metric_c):
    stiffness = gamma_gas * pressure_c
    sound = jnp.sqrt(stiffness / density_c)
    signs = jnp.concatenate([-jnp.ones((64,), jnp.float32), jnp.ones((64,), jnp.float32)])
    pieces = []
    for direction in range(3):
        block_in = difference[:, :, 128 * direction : 128 * direction + 128]
        flux_out = adjoint_flux(block_in, direction, density_c, velocity_c[direction], stiffness)
        speed = jnp.abs(velocity_c[direction]) + sound
        pieces.append(
            0.5
            * lift_end
            * metric_c[direction][..., None]
            * (signs * flux_out + speed[..., None] * block_in)
        )
    return jnp.concatenate(pieces, axis=2)


def on_device(
    adjoint, density, velocity, pressure, metric, face_source, face_flip, face_tag, send_list
):
    highest = lax.Precision.HIGHEST
    element_count = adjoint.shape[0]
    columns = face_source.shape[0]
    layers = element_count // columns
    derivative_matrix = jnp.asarray(derivative_tables(), jnp.float32)
    picker = jnp.asarray(face_table(), jnp.float32)
    picker_back = jnp.asarray(np.transpose(face_table()), jnp.float32)
    mirror = jnp.asarray(mirror_table(), jnp.float32)
    wall_sign = jnp.asarray(wall_table(columns), jnp.float32)
    flip_mask = (face_flip.reshape(-1) == 1)[None, :, None]
    tag_mask = face_tag.reshape(-1)[None, :, None]
    sources = face_source.reshape(-1)
    density_c = density[:, None]
    velocity_c = [velocity[direction][:, None] for direction in range(3)]
    pressure_c = pressure[:, None]
    metric_c = [metric[direction][:, None] for direction in range(3)]

    def residual(current):
        rows_flat = current.reshape(element_count * 5, 512)
        traces = jnp.dot(
            rows_flat, picker, precision=highest, preferred_element_type=jnp.float32
        ).reshape(element_count, 5, 384)
        in_plane = jnp.swapaxes(traces[:, :, :256].reshape(element_count, 5, 4, 64), 1, 2).reshape(
            layers, 4 * columns, 320
        )
        lower_faces = traces[:, :, 256:320].reshape(layers, columns, 320)
        upper_faces = traces[:, :, 320:].reshape(layers, columns, 320)
        passed = [
            passed_along(outgoing, "span", offset)
            for offset, outgoing in ((1, upper_faces[layers - 1]), (-1, lower_faces[0]))
        ]
        from_below = passed[0]
        from_above = passed[1]
        packets = [jnp.take(in_plane, send_list[row_index], axis=1) for row_index in range(4)]
        arrived = [
            passed_along(packets[row_index], "elem", offset)
            for row_index, offset in enumerate((1, 2, -1, -2))
        ]
        source_rows = jnp.concatenate([in_plane] + arrived, axis=1)
        exterior = jnp.take(source_rows, sources, axis=1)
        mirrored = jnp.dot(exterior, mirror, precision=highest, preferred_element_type=jnp.float32)
        exterior = jnp.where(flip_mask, mirrored, exterior)
        exterior = jnp.where(
            tag_mask == 0,
            exterior,
            jnp.where(tag_mask == 1, in_plane * wall_sign, jnp.zeros_like(exterior)),
        )
        outer_plane = jnp.swapaxes(exterior.reshape(element_count, 4, 5, 64), 1, 2).reshape(
            element_count, 5, 256
        )
        outer_lower = jnp.concatenate([from_below[None], upper_faces[:-1]], axis=0).reshape(
            element_count, 5, 64
        )
        outer_upper = jnp.concatenate([lower_faces[1:], from_above[None]], axis=0).reshape(
            element_count, 5, 64
        )
        difference = jnp.concatenate([outer_plane, outer_lower, outer_upper], axis=2) - traces
        surface = face_terms(difference, density_c, velocity_c, pressure_c, metric_c)
        derivatives = jnp.dot(
            rows_flat, derivative_matrix, precision=highest, preferred_element_type=jnp.float32
        ).reshape(element_count, 5, 3, 512)
        volume = volume_terms(
            [derivatives[:, :, direction, :] for direction in range(3)],
            density_c,
            velocity_c,
            pressure_c,
            metric_c,
        )
        lifted = jnp.dot(
            surface.reshape(element_count * 5, 384),
            picker_back,
            precision=highest,
            preferred_element_type=jnp.float32,
        ).reshape(element_count, 5, 512)
        return volume + lifted

    section_one = time_step * residual(adjoint)
    middle = adjoint + section_b1 * section_one
    register = section_a2 * section_one + time_step * residual(middle)
    return (middle + section_b2 * register, register)


def solution(mesh):
    placed = (
        P(("span", "elem"), None, None),
        P(("span", "elem")),
        P(None, ("span", "elem")),
        P(("span", "elem")),
        P(None, ("span", "elem")),
        P("elem", None),
        P("elem", None),
        P("elem", None),
        P("elem", None),
    )
    return jax.shard_map(
        on_device,
        mesh=mesh,
        in_specs=placed,
        out_specs=(P(("span", "elem"), None, None), P(("span", "elem"), None, None)),
        check_vma=False,
    )
```

profile of v0, /device:TPU:1, one launch (start us, length us, event | category | flops | bytes accessed | tf_op | source)
XLA Modules:
  0.0 120.4 jit_solution(11331039215262694227)
XLA Ops:
  0.6 1.0 slice_reduce_fusion
  1.7 1.8 %convolution_bitcast_fusion.1 = f32[16,5,384]{2,0,1:T(8,128)S(1)} fusion(f32[512,384,1]{1,0,2:T(8,128)} %constant.71, f32[16,5,512]{2,0,1:T(8,128)} %param.18), kind=kOutput, calls=%fused_computation.17 | convolution fusion | flops 188743680 | bytes 1073152 | tf_op jit(solution)/shard_map/dot_general | solution.py:145
  5.9 4.4 %collective-permute-start = (f32[4,2,320]{2,0,1:T(4,128)}, f32[4,2,320]{2,0,1:T(4,128)}, u32[]{:S(2)}, u32[]{:S(2)}) collective-permute-start(f32[4,2,320]{2,0,1:T(4,128)} %select_bitcast_fusion.7), channel_id=1, source_target_pairs={{1016,0},{0,8},{8,16},{16,24},{24,32},{32,40},{40,48},{48,56},{56,... | collective-permute-start | bytes 30728 | tf_op jit(solution)/shard_map/ppermute | solution.py:18
  11.5 4.9 %collective-permute-start.1 = (f32[4,2,320]{2,0,1:T(4,128)}, f32[4,2,320]{2,0,1:T(4,128)}, u32[]{:S(2)}, u32[]{:S(2)}) collective-permute-start(f32[4,2,320]{2,0,1:T(4,128)} %select_bitcast_fusion.6), channel_id=1, source_target_pairs={{1008,0},{1016,8},{0,16},{8,24},{16,32},{24,40},{32,48},{40,56},{4... | collective-permute-start | bytes 30728 | tf_op jit(solution)/shard_map/ppermute | solution.py:18
  17.7 16.0 %collective-permute-start.2 = (f32[4,2,320]{2,0,1:T(4,128)}, f32[4,2,320]{2,0,1:T(4,128)}, u32[]{:S(2)}, u32[]{:S(2)}) collective-permute-start(f32[4,2,320]{2,0,1:T(4,128)} %select_bitcast_fusion.5), channel_id=1, source_target_pairs={{8,0},{16,8},{24,16},{32,24},{40,32},{48,40},{56,48},{64,56},{72,6... | collective-permute-start | bytes 30728 | tf_op jit(solution)/shard_map/ppermute | solution.py:18
  35.0 4.3 %collective-permute-start.3 = (f32[4,2,320]{2,0,1:T(4,128)}, f32[4,2,320]{2,0,1:T(4,128)}, u32[]{:S(2)}, u32[]{:S(2)}) collective-permute-start(f32[4,2,320]{2,0,1:T(4,128)} %select_bitcast_fusion.4), channel_id=1, source_target_pairs={{16,0},{24,8},{32,16},{40,24},{48,32},{56,40},{64,48},{72,56},{80,... | collective-permute-start | bytes 30728 | tf_op jit(solution)/shard_map/ppermute | solution.py:18
  40.0 2.7 %collective-permute-start.4 = (f32[4,320]{1,0:T(4,128)}, f32[4,320]{1,0:T(4,128)}, u32[]{:S(2)}, u32[]{:S(2)}) collective-permute-start(f32[4,320]{1,0:T(4,128)} %squeeze.35), channel_id=1, source_target_pairs={{7,0},{0,1},{1,2},{2,3},{3,4},{4,5},{5,6},{6,7},{15,8},{8,9},{9,10... | collective-permute-start | bytes 15368 | tf_op jit(solution)/shard_map/ppermute | solution.py:18
  45.6 5.0 %convolution_bitcast_fusion = f32[16,5,3,512]{3,0,1,2:T(8,128)S(1)} fusion(f32[3,512,512,1]{2,1,3,0:T(8,128)} %constant.70, f32[16,5,512]{2,0,1:T(8,128)S(1)} %copy-done.4), kind=kOutput, calls=%fused_computation.10 | convolution fusion | flops 754974720 | bytes 3801088 | tf_op jit(solution)/shard_map/dot_general | solution.py:184
  59.8 2.3 %collective-permute-done.5 = f32[4,320]{1,0:T(4,128)S(1)} collective-permute-done((f32[4,320]{1,0:T(4,128)S(1)}, f32[4,320]{1,0:T(4,128)S(1)}, u32[]{:S(2)}, u32[]{:S(2)}) %collective-permute-start.5) | collective-permute-done | bytes 5152 | tf_op jit(solution)/shard_map/ppermute | solution.py:18
  63.5 0.8 reshape.739
  64.9 1.3 %constant_dynamic-update-slice_fusion.18 = f32[4,24,320]{2,0,1:T(4,128)} fusion(f32[4,24,320]{2,0,1:T(4,128)} %get-tuple-element.59, f32[4,2,320]{2,0,1:T(4,128)} %collective-permute-done), kind=kLoop, calls=%fused_computation.51 | loop fusion | bytes 24576
  66.2 1.3 %constant_dynamic-update-slice_fusion.17 = f32[4,24,320]{2,0,1:T(4,128)} fusion(f32[4,24,320]{2,0,1:T(4,128)} %constant_dynamic-update-slice_fusion.18, f32[4,2,320]{2,0,1:T(4,128)} %collective-permute-done.1), kind=kLoop, calls=%fused_computation.50 | loop fusion | bytes 24576
  67.5 1.3 %constant_dynamic-update-slice_fusion.16 = f32[4,24,320]{2,0,1:T(4,128)} fusion(f32[4,24,320]{2,0,1:T(4,128)} %constant_dynamic-update-slice_fusion.17, f32[4,2,320]{2,0,1:T(4,128)} %collective-permute-done.2), kind=kLoop, calls=%fused_computation.49 | loop fusion | bytes 24576
  68.9 1.3 %constant_dynamic-update-slice_fusion.15 = f32[4,24,320]{2,0,1:T(4,128)} fusion(f32[4,24,320]{2,0,1:T(4,128)} %constant_dynamic-update-slice_fusion.16, f32[4,2,320]{2,0,1:T(4,128)} %collective-permute-done.3), kind=kLoop, calls=%fused_computation.48 | loop fusion | bytes 24576 | tf_op jit(solution)/shard_map/concatenate | solution.py:164
  70.2 2.3 %gather_fusion.4 = f32[16,4,320]{2,1,0:T(4,128)} fusion(f32[4,24,320]{2,0,1:T(4,128)} %constant_dynamic-update-slice_fusion.15, s32[1024]{0:T(1024)} %pad_clamp_fusion), kind=kCustom, calls=%fused_computation.1.clone | custom fusion | bytes 163904 | tf_op jit(solution)/shard_map/jit(_take)/gather | solution.py:165
  72.4 2.3 %fusion.2 = f32[4,16,320]{2,1,0:T(8,128)} fusion(f32[320,320,1]{1,0,2:T(8,128)} %constant.72, f32[16,4,320]{2,1,0:T(4,128)} %gather_fusion.4, f32[4,16,320]{2,1,0:T(8,128)} %copy-done.5, f32[16,320]{1,0:T(8,128)} %constant.58.clone, pred[16]{0:T(512)(128)(4,1)} %compare_and_fusion, pred[16]{0:T(512)(128)(4,1)} %eq.39, pred[16]{0:T(512)(128)(4,1)} %eq.37, ...), kind=kOutput, calls=%fused_computation.18 | convolution fusion | flops 78766080 | bytes 675904 | tf_op jit(solution)/shard_map/dot_general | solution.py:166
  74.7 1.7 %reshape.736 = f32[16,4,5,64]{3,2,1,0:T(8,128)} reshape(f32[4,16,320]{2,1,0:T(8,128)} %fusion.2) | data formatting | bytes 163840 | tf_op jit(solution)/shard_map/reshape | solution.py:173
  76.4 1.7 %copy.30 = f32[16,5,4,64]{3,2,0,1:T(4,128)} copy(f32[16,5,4,64]{3,1,2,0:T(8,128)} %bitcast.105) | data formatting | bytes 163840 | tf_op jit(solution)/shard_map/transpose | solution.py:173
  78.1 1.1 reshape.737
  79.1 0.9 maximum_subtract_fusion
  80.3 0.8 constant_dynamic-update-slice_fusion.23
  82.1 2.7 %multiply_add_fusion.1 = (f32[16,5,512]{2,0,1:T(8,128)S(1)}, f32[16,5,512]{2,0,1:T(8,128)}) fusion(f32[16,5,512]{2,0,1:T(8,128)S(1)} %copy-done.4, f32[384,512,1]{1,0,2:T(8,128)} %constant.73, f32[16,5,128]{2,0,1:T(8,128)S(1)} %get-tuple-element.29, f32[16,5,128]{2,0,1:T(8,128)S(1)} %get-tuple-element.30, f32[16,5,128]{2,0,1:T(8,128)S(1)} %get-tuple-element.28, ...), kind=kOutput, calls=%fused_computation.29 | convolution fusion | flops 189132800 | bytes 1892544 | tf_op jit(solution)/shard_map/dot_general | solution.py:194
  84.9 3.9 %fusion.4 = f32[16,5,3,512]{3,0,1,2:T(8,128)} fusion(f32[3,512,512,1]{2,1,3,0:T(8,128)S(1)} %copy-done, f32[16,5,512]{2,0,1:T(8,128)S(1)} %get-tuple-element.86), kind=kOutput, calls=%fused_computation.30 | convolution fusion | flops 754974720 | bytes 3801088 | tf_op jit(solution)/shard_map/dot_general | solution.py:184
  92.8 1.2 slice_bitcast_fusion.2
  94.9 2.2 %collective-permute-start.6 = (f32[4,2,320]{2,0,1:T(4,128)S(1)}, f32[4,2,320]{2,0,1:T(4,128)S(1)}, u32[]{:S(2)}, u32[]{:S(2)}) collective-permute-start(f32[4,2,320]{2,0,1:T(4,128)S(1)} %select_bitcast_fusion.3), channel_id=1, source_target_pairs={{1016,0},{0,8},{8,16},{16,24},{24,32},{32,40},{40,48},{48,56},{56,... | collective-permute-start | bytes 30728 | tf_op jit(solution)/shard_map/ppermute | solution.py:18
  97.2 1.9 %collective-permute-start.7 = (f32[4,2,320]{2,0,1:T(4,128)S(1)}, f32[4,2,320]{2,0,1:T(4,128)S(1)}, u32[]{:S(2)}, u32[]{:S(2)}) collective-permute-start(f32[4,2,320]{2,0,1:T(4,128)S(1)} %select_bitcast_fusion.2), channel_id=1, source_target_pairs={{1008,0},{1016,8},{0,16},{8,24},{16,32},{24,40},{32,48},{40,56},{4... | collective-permute-start | bytes 30728 | tf_op jit(solution)/shard_map/ppermute | solution.py:18
  99.2 6.4 %collective-permute-start.8 = (f32[4,2,320]{2,0,1:T(4,128)S(1)}, f32[4,2,320]{2,0,1:T(4,128)S(1)}, u32[]{:S(2)}, u32[]{:S(2)}) collective-permute-start(f32[4,2,320]{2,0,1:T(4,128)S(1)} %select_bitcast_fusion.1), channel_id=1, source_target_pairs={{8,0},{16,8},{24,16},{32,24},{40,32},{48,40},{56,48},{64,56},{72,6... | collective-permute-start | bytes 30728 | tf_op jit(solution)/shard_map/ppermute | solution.py:18
  105.7 4.2 %collective-permute-start.9 = (f32[4,2,320]{2,0,1:T(4,128)S(1)}, f32[4,2,320]{2,0,1:T(4,128)S(1)}, u32[]{:S(2)}, u32[]{:S(2)}) collective-permute-start(f32[4,2,320]{2,0,1:T(4,128)S(1)} %select_bitcast_fusion), channel_id=1, source_target_pairs={{16,0},{24,8},{32,16},{40,24},{48,32},{56,40},{64,48},{72,56},{80,... | collective-permute-start | bytes 30728 | tf_op jit(solution)/shard_map/ppermute | solution.py:18
  110.0 1.2 collective-permute-start.10
  111.9 3.5 %collective-permute-start.11 = (f32[4,320]{1,0:T(4,128)S(1)}, f32[4,320]{1,0:T(4,128)S(1)}, u32[]{:S(2)}, u32[]{:S(2)}) collective-permute-start(f32[4,320]{1,0:T(4,128)S(1)} %squeeze.41), channel_id=1, source_target_pairs={{1,0},{2,1},{3,2},{4,3},{5,4},{6,5},{7,6},{0,7},{9,8},{10,9},{11,1... | collective-permute-start | bytes 15368 | tf_op jit(solution)/shard_map/ppermute | solution.py:18
  115.5 0.8 collective-permute-done.11
  119.0 1.4 %multiply_add_fusion = (f32[16,5,512]{2,0,1:T(8,128)}, f32[16,5,512]{2,0,1:T(8,128)}) fusion(f32[16,5,512]{2,0,1:T(8,128)S(1)} %get-tuple-element.86, f32[384,512,1]{1,0,2:T(8,128)S(1)} %copy-done.1, f32[16,5,128]{2,0,1:T(8,128)S(1)} %get-tuple-element.23, f32[16,5,128]{2,0,1:T(8,128)S(1)} %get-tuple-element.24, f32[16,5,128]{2,0,1:T(8,128)S(1)} %get-tuple-element.22, ...), kind=kOutput, calls=%fused_computation.28 | convolution fusion | flops 189255680 | bytes 2056384 | tf_op jit(solution)/shard_map/dot_general | solution.py:194
  (263 shorter events, 30.2 us)
Async XLA Ops:
  0.6 44.9 %copy-start.4 = (f32[16,5,512]{2,0,1:T(8,128)S(1)}, f32[16,5,512]{2,0,1:T(8,128)}, u32[]{:S(2)}) copy-start(f32[16,5,512]{2,0,1:T(8,128)} %param.18) | copy-start | bytes 491524
  1.7 33.3 %copy-start.51 = (pred[2]{0:T(512)(128)(4,1)}, pred[2]{0:T(512)(128)(4,1)S(1)}, u32[]{:S(2)}) copy-start(pred[2]{0:T(512)(128)(4,1)S(1)} %compare_and_fusion.4) | copy-start | bytes 10
  3.8 47.3 %copy-start.20 = (f32[16]{0:T(128)S(1)}, f32[16]{0:T(128)}, u32[]{:S(2)}) copy-start(f32[16]{0:T(128)} %param.19) | copy-start | bytes 196
  3.8 47.3 %copy-start.42 = (f32[3,16]{1,0:T(4,128)S(1)}, f32[3,16]{1,0:T(4,128)}, u32[]{:S(2)}) copy-start(f32[3,16]{1,0:T(4,128)} %param.20) | copy-start | bytes 580
  3.8 47.3 %copy-start.61 = (f32[16]{0:T(128)S(1)}, f32[16]{0:T(128)}, u32[]{:S(2)}) copy-start(f32[16]{0:T(128)} %param.21) | copy-start | bytes 196
  3.9 40.8 %copy-start.5 = (f32[4,16,320]{2,1,0:T(8,128)}, f32[4,16,320]{2,1,0:T(8,128)S(1)}, u32[]{:S(2)}) copy-start(f32[4,16,320]{2,1,0:T(8,128)S(1)} %reshape.734) | copy-start | bytes 245764
  4.6 47.3 %copy-start.60 = (s32[4,4]{1,0:T(4,128)S(1)}, s32[4,4]{1,0:T(4,128)}, u32[]{:S(2)}) copy-start(s32[4,4]{1,0:T(4,128)} %param.25) | copy-start | bytes 196
  4.6 47.3 %copy-start.59 = (s32[4,4]{1,0:T(4,128)S(1)}, s32[4,4]{1,0:T(4,128)}, u32[]{:S(2)}) copy-start(s32[4,4]{1,0:T(4,128)} %param.24) | copy-start | bytes 196
  4.6 47.3 %copy-start.41 = (f32[3,16]{1,0:T(4,128)S(1)}, f32[3,16]{1,0:T(4,128)}, u32[]{:S(2)}) copy-start(f32[3,16]{1,0:T(4,128)} %param.22) | copy-start | bytes 580
  4.6 40.1 %copy-start.25 = (s32[1024]{0:T(1024)}, s32[1024]{0:T(1024)S(1)}, u32[]{:S(2)}) copy-start(s32[1024]{0:T(1024)S(1)} %get-tuple-element.92) | copy-start | bytes 12292
  4.6 40.1 %copy-start.26 = (s32[1024]{0:T(1024)}, s32[1024]{0:T(1024)S(1)}, u32[]{:S(2)}) copy-start(s32[1024]{0:T(1024)S(1)} %get-tuple-element.93) | copy-start | bytes 12292
  5.9 59.1 %collective-permute-start = (f32[4,2,320]{2,0,1:T(4,128)}, f32[4,2,320]{2,0,1:T(4,128)}, u32[]{:S(2)}, u32[]{:S(2)}) collective-permute-start(f32[4,2,320]{2,0,1:T(4,128)} %select_bitcast_fusion.7), channel_id=1, source_target_pairs={{1016,0},{0,8},{8,16},{16,24},{24,32},{32,40},{40,48},{48,56},{56,... | collective-permute-start | bytes 30728 | tf_op jit(solution)/shard_map/ppermute | solution.py:18
  11.5 54.7 %collective-permute-start.1 = (f32[4,2,320]{2,0,1:T(4,128)}, f32[4,2,320]{2,0,1:T(4,128)}, u32[]{:S(2)}, u32[]{:S(2)}) collective-permute-start(f32[4,2,320]{2,0,1:T(4,128)} %select_bitcast_fusion.6), channel_id=1, source_target_pairs={{1008,0},{1016,8},{0,16},{8,24},{16,32},{24,40},{32,48},{40,56},{4... | collective-permute-start | bytes 30728 | tf_op jit(solution)/shard_map/ppermute | solution.py:18
  16.5 28.3 %copy-start.27 = (s32[1024]{0:T(1024)}, s32[1024]{0:T(1024)S(1)}, u32[]{:S(2)}) copy-start(s32[1024]{0:T(1024)S(1)} %get-tuple-element.90) | copy-start | bytes 12292
  17.7 49.8 %collective-permute-start.2 = (f32[4,2,320]{2,0,1:T(4,128)}, f32[4,2,320]{2,0,1:T(4,128)}, u32[]{:S(2)}, u32[]{:S(2)}) collective-permute-start(f32[4,2,320]{2,0,1:T(4,128)} %select_bitcast_fusion.5), channel_id=1, source_target_pairs={{8,0},{16,8},{24,16},{32,24},{40,32},{48,40},{56,48},{64,56},{72,6... | collective-permute-start | bytes 30728 | tf_op jit(solution)/shard_map/ppermute | solution.py:18
  35.0 33.9 %collective-permute-start.3 = (f32[4,2,320]{2,0,1:T(4,128)}, f32[4,2,320]{2,0,1:T(4,128)}, u32[]{:S(2)}, u32[]{:S(2)}) collective-permute-start(f32[4,2,320]{2,0,1:T(4,128)} %select_bitcast_fusion.4), channel_id=1, source_target_pairs={{16,0},{24,8},{32,16},{40,24},{48,32},{56,40},{64,48},{72,56},{80,... | collective-permute-start | bytes 30728 | tf_op jit(solution)/shard_map/ppermute | solution.py:18
  40.0 19.1 %collective-permute-start.4 = (f32[4,320]{1,0:T(4,128)}, f32[4,320]{1,0:T(4,128)}, u32[]{:S(2)}, u32[]{:S(2)}) collective-permute-start(f32[4,320]{1,0:T(4,128)} %squeeze.35), channel_id=1, source_target_pairs={{7,0},{0,1},{1,2},{2,3},{3,4},{4,5},{5,6},{6,7},{15,8},{8,9},{9,10... | collective-permute-start | bytes 15368 | tf_op jit(solution)/shard_map/ppermute | solution.py:18
  50.6 29.6 %copy-start.21 = (f32[16]{0:T(128)S(1)}, f32[16]{0:T(128)}, u32[]{:S(2)}) copy-start(f32[16]{0:T(128)} %param.19) | copy-start | bytes 196
  53.2 31.7 %copy-start = (f32[3,512,512,1]{2,1,3,0:T(8,128)S(1)}, f32[3,512,512,1]{2,1,3,0:T(8,128)}, u32[]{:S(2)}) copy-start(f32[3,512,512,1]{2,1,3,0:T(8,128)} %constant.70) | copy-start | bytes 9437188
  59.1 3.1 %collective-permute-start.5 = (f32[4,320]{1,0:T(4,128)S(1)}, f32[4,320]{1,0:T(4,128)S(1)}, u32[]{:S(2)}, u32[]{:S(2)}) collective-permute-start(f32[4,320]{1,0:T(4,128)S(1)} %squeeze.36), channel_id=1, source_target_pairs={{1,0},{2,1},{3,2},{4,3},{5,4},{6,5},{7,6},{0,7},{9,8},{10,9},{11,1... | collective-permute-start | bytes 15368 | tf_op jit(solution)/shard_map/ppermute | solution.py:18
  88.8 28.5 %copy-start.3 = (f32[320,320,1]{1,0,2:T(8,128)S(1)}, f32[320,320,1]{1,0,2:T(8,128)}, u32[]{:S(2)}) copy-start(f32[320,320,1]{1,0,2:T(8,128)} %constant.72) | copy-start | bytes 1228804
  88.8 28.5 %copy-start.19 = (f32[16,320]{1,0:T(8,128)S(1)}, f32[16,320]{1,0:T(8,128)}, u32[]{:S(2)}) copy-start(f32[16,320]{1,0:T(8,128)} %constant.58.clone) | copy-start | bytes 61444
  88.9 28.5 %copy-start.47 = (pred[16]{0:T(512)(128)(4,1)S(1)}, pred[16]{0:T(512)(128)(4,1)}, u32[]{:S(2)}) copy-start(pred[16]{0:T(512)(128)(4,1)} %compare_and_fusion) | copy-start | bytes 52
  88.9 28.5 %copy-start.48 = (pred[16]{0:T(512)(128)(4,1)S(1)}, pred[16]{0:T(512)(128)(4,1)}, u32[]{:S(2)}) copy-start(pred[16]{0:T(512)(128)(4,1)} %eq.35) | copy-start | bytes 52
  88.9 28.5 %copy-start.49 = (pred[16]{0:T(512)(128)(4,1)S(1)}, pred[16]{0:T(512)(128)(4,1)}, u32[]{:S(2)}) copy-start(pred[16]{0:T(512)(128)(4,1)} %eq.39) | copy-start | bytes 52
  88.9 28.5 %copy-start.50 = (pred[16]{0:T(512)(128)(4,1)S(1)}, pred[16]{0:T(512)(128)(4,1)}, u32[]{:S(2)}) copy-start(pred[16]{0:T(512)(128)(4,1)} %eq.37) | copy-start | bytes 52
  94.9 21.6 %collective-permute-start.6 = (f32[4,2,320]{2,0,1:T(4,128)S(1)}, f32[4,2,320]{2,0,1:T(4,128)S(1)}, u32[]{:S(2)}, u32[]{:S(2)}) collective-permute-start(f32[4,2,320]{2,0,1:T(4,128)S(1)} %select_bitcast_fusion.3), channel_id=1, source_target_pairs={{1016,0},{0,8},{8,16},{16,24},{24,32},{32,40},{40,48},{48,56},{56,... | collective-permute-start | bytes 30728 | tf_op jit(solution)/shard_map/ppermute | solution.py:18
  97.2 19.3 %collective-permute-start.7 = (f32[4,2,320]{2,0,1:T(4,128)S(1)}, f32[4,2,320]{2,0,1:T(4,128)S(1)}, u32[]{:S(2)}, u32[]{:S(2)}) collective-permute-start(f32[4,2,320]{2,0,1:T(4,128)S(1)} %select_bitcast_fusion.2), channel_id=1, source_target_pairs={{1008,0},{1016,8},{0,16},{8,24},{16,32},{24,40},{32,48},{40,56},{4... | collective-permute-start | bytes 30728 | tf_op jit(solution)/shard_map/ppermute | solution.py:18
  99.2 17.4 %collective-permute-start.8 = (f32[4,2,320]{2,0,1:T(4,128)S(1)}, f32[4,2,320]{2,0,1:T(4,128)S(1)}, u32[]{:S(2)}, u32[]{:S(2)}) collective-permute-start(f32[4,2,320]{2,0,1:T(4,128)S(1)} %select_bitcast_fusion.1), channel_id=1, source_target_pairs={{8,0},{16,8},{24,16},{32,24},{40,32},{48,40},{56,48},{64,56},{72,6... | collective-permute-start | bytes 30728 | tf_op jit(solution)/shard_map/ppermute | solution.py:18
  105.7 10.9 %collective-permute-start.9 = (f32[4,2,320]{2,0,1:T(4,128)S(1)}, f32[4,2,320]{2,0,1:T(4,128)S(1)}, u32[]{:S(2)}, u32[]{:S(2)}) collective-permute-start(f32[4,2,320]{2,0,1:T(4,128)S(1)} %select_bitcast_fusion), channel_id=1, source_target_pairs={{16,0},{24,8},{32,16},{40,24},{48,32},{56,40},{64,48},{72,56},{80,... | collective-permute-start | bytes 30728 | tf_op jit(solution)/shard_map/ppermute | solution.py:18
  110.0 1.9 %collective-permute-start.10 = (f32[4,320]{1,0:T(4,128)S(1)}, f32[4,320]{1,0:T(4,128)S(1)}, u32[]{:S(2)}, u32[]{:S(2)}) collective-permute-start(f32[4,320]{1,0:T(4,128)S(1)} %squeeze.40), channel_id=1, source_target_pairs={{7,0},{0,1},{1,2},{2,3},{3,4},{4,5},{5,6},{6,7},{15,8},{8,9},{9,10... | collective-permute-start | bytes 15368 | tf_op jit(solution)/shard_map/ppermute | solution.py:18
  111.9 4.4 %collective-permute-start.11 = (f32[4,320]{1,0:T(4,128)S(1)}, f32[4,320]{1,0:T(4,128)S(1)}, u32[]{:S(2)}, u32[]{:S(2)}) collective-permute-start(f32[4,320]{1,0:T(4,128)S(1)} %squeeze.41), channel_id=1, source_target_pairs={{1,0},{2,1},{3,2},{4,3},{5,4},{6,5},{7,6},{0,7},{9,8},{10,9},{11,1... | collective-permute-start | bytes 15368 | tf_op jit(solution)/shard_map/ppermute | solution.py:18
  (42 other events, 712.1 us)
where the time goes:
time: 122 us; the launch traced here: 120 us
  starting transfers between devices  51.6 us (42%)
  local copies, waits for them, and re-layouts  33.6 us (28%)
  matrix products  18.1 us (15%)
  other arithmetic  11.9 us (10%)
  waiting for transfers between devices  3.48 us (3%)
  between operations  1.67 us (1%)
    ppermute x12, starting transfers between devices, passed_along(): return lax.ppermute(block, axis, route)  51.6 us
    dot_general x2, matrix products, residual(): jnp.dot(rows_flat, derivative_matrix, precision=highest, preferred_elemen...  8.99 us
    gather x8, local copies, waits for them, and re-layouts, residual(): jnp.take(in_plane, send_list[row_index], axis=1)  5.06 us
    unnamed x130, local copies, waits for them, and re-layouts  5.01 us
    dot_general x2, matrix products, residual(): jnp.dot(surface.reshape(element_count * 5, 384), picker_back, precision=h...  4.06 us
    ppermute x12, waiting for transfers between devices, passed_along(): return lax.ppermute(block, axis, route)  3.48 us
    unnamed x31, other arithmetic  3.04 us
    gather x2, local copies, waits for them, and re-layouts, residual(): exterior = jnp.take(source_rows, sources, axis=1)  3.02 us
  transfers between devices with their start and end apart: 12, of which 3 were waited for; matrix products, arithmetic and copies ran while one was open for 23% of the time, Pallas kernels for 0%

commit v1 on v0

v1 whole, which is shorter than its diff:
```python
import functools

import jax
import jax.numpy as jnp
import numpy as np
from jax import lax
from jax.experimental import pallas as pl
from jax.experimental.pallas import tpu as pltpu
from jax.sharding import PartitionSpec as P

gamma_gas = 1.4
lift_end = 28.0
time_step = 0.02
section_a2 = -567301805773.0 / 1357537059087.0
section_b1 = 1432997174477.0 / 9575080441755.0
section_b2 = 5161836677717.0 / 13612068292357.0
offsets = (1, 2, -1, -2)
MESH = pl.DeviceIdType.MESH


def lobatto_derivative():
    positions = np.array(
        [
            -1.0,
            -0.8717401485096066,
            -0.5917001814331423,
            -0.2092992179024789,
            0.2092992179024789,
            0.5917001814331423,
            0.8717401485096066,
            1.0,
        ]
    )
    total_nodes = positions.shape[0]
    differences = positions[:, None] - positions[None, :] + np.eye(total_nodes)
    weights = 1.0 / np.prod(differences, axis=1)
    matrix_out = weights[None, :] / weights[:, None] / differences
    matrix_out = matrix_out * (1.0 - np.eye(total_nodes))
    return matrix_out - np.eye(total_nodes) * np.sum(matrix_out, axis=1)[:, None]


def plane_table():
    matrix_in = lobatto_derivative()
    along_x = np.kron(np.eye(16), matrix_in).T
    along_y = np.kron(np.eye(2), np.kron(matrix_in, np.eye(8))).T
    table = np.concatenate([along_x, along_y], axis=1).astype(np.float32)
    high = table.astype(jnp.bfloat16)
    low = (table - high.astype(np.float32)).astype(jnp.bfloat16)
    return np.concatenate([high, high, low], axis=0)


def depth_table():
    matrix_in = lobatto_derivative()
    table = np.zeros((4, 4, 2, 128))
    for out_tile in range(4):
        for in_tile in range(4):
            table[out_tile, in_tile, 0, :64] = matrix_in[2 * out_tile, 2 * in_tile]
            table[out_tile, in_tile, 0, 64:] = matrix_in[2 * out_tile + 1, 2 * in_tile + 1]
            table[out_tile, in_tile, 1, :64] = matrix_in[2 * out_tile, 2 * in_tile + 1]
            table[out_tile, in_tile, 1, 64:] = matrix_in[2 * out_tile + 1, 2 * in_tile]
    return table.reshape(32, 128).astype(np.float32)


def along_axis(values, index, axis):
    rest = tuple(a for a in range(values.ndim) if a != axis)
    numbers = lax.GatherDimensionNumbers(
        offset_dims=(),
        collapsed_slice_dims=(axis,),
        start_index_map=(axis,),
        operand_batching_dims=rest,
        start_indices_batching_dims=rest,
    )
    index = jnp.broadcast_to(index, values.shape)
    return lax.gather(
        values,
        index[..., None],
        numbers,
        slice_sizes=(1,) * values.ndim,
        mode=lax.GatherScatterMode.PROMISE_IN_BOUNDS,
    )


def lanes(values, index):
    return along_axis(values, index, values.ndim - 1)


def rows(values, index):
    return along_axis(values, index, values.ndim - 2)


def kernel(
    adj_hbm, rho_hbm, vel_hbm, pres_hbm, met_hbm, src_hbm, flip_hbm, tag_hbm, send_hbm, plane_hbm, depth_hbm,
    next_hbm, reg_hbm,
    q_ref, mid_ref, keep_ref, acc_ref, out_ref,
    rho_ref, vel_ref, pres_ref, met_ref, src_ref, flip_ref, tag_ref, send_ref, plane_ref, depth_ref,
    tx_ref, tz_ref, rx_ref, rz_ref,
    in_sem, out_sem, tx_sem, rx_sem,
):
    n_elem, n_span = lax.axis_size("elem"), lax.axis_size("span")
    part, slab = lax.axis_index("elem"), lax.axis_index("span")
    peers = [{"elem": lax.rem(part + n_elem + o, n_elem)} for o in offsets]
    peers += [{"span": lax.rem(slab + n_span + o, n_span)} for o in (1, -1)]

    barrier = pltpu.get_barrier_semaphore()
    for peer in peers:
        pl.semaphore_signal(barrier, inc=1, device_id=peer, device_id_type=MESH)

    loads = [
        pltpu.make_async_copy(src, dst, in_sem.at[i])
        for i, (src, dst) in enumerate(
            [
                (send_hbm, send_ref), (adj_hbm, q_ref), (plane_hbm, plane_ref), (depth_hbm, depth_ref),
                (rho_hbm, rho_ref), (vel_hbm, vel_ref), (pres_hbm, pres_ref), (met_hbm, met_ref),
                (src_hbm, src_ref), (flip_hbm, flip_ref), (tag_hbm, tag_ref),
            ]
        )
    ]
    for load in loads:
        load.start()

    lane = lax.broadcasted_iota(jnp.int32, (8, 128), 1)
    row = lax.broadcasted_iota(jnp.int32, (8, 128), 0)
    half, place = lane >> 6, lane & 63
    first_half = half == 0
    low_rows = row < 4
    column, group = row & 3, row & 4
    from_x = ((lane >> 3) & 1) * 64 + (lane & 7) * 8 + 7 * half
    from_y = ((lane >> 3) & 1) * 64 + 56 * half + (lane & 7)
    quarter = place >> 4
    node_i, node_j, node_k = lane & 7, (lane >> 3) & 7, lane >> 6
    to_x = 64 * (node_i >> 2) + 8 * node_k + node_j
    to_y = 64 * (node_j >> 2) + 8 * node_k + node_i
    on_x = (node_i == 0) | (node_i == 7)
    on_y = (node_j == 0) | (node_j == 7)

    def tiles_of(ref):
        return [ref[:, :, 128 * t : 128 * t + 128].reshape(10, 8, 128) for t in range(4)]

    def traces(q):
        pair_x, pair_y = lanes(q[0], from_x), lanes(q[0], from_y)
        for t in range(1, 4):
            pair_x = jnp.where(quarter == t, lanes(q[t], from_x), pair_x)
            pair_y = jnp.where(quarter == t, lanes(q[t], from_y), pair_y)
        return pair_x, pair_y, jnp.where(first_half, q[0], q[3])

    def picked(pair_x, pair_y, face):
        index = group + ((face >> 2) & 3)
        return jnp.where((face & 2) == 0, rows(pair_x, index), rows(pair_y, index))

    def send(pair_x, pair_y, swapped, turned, send_faces, turn):
        outs = [
            lanes(picked(pair_x, pair_y, face), 64 * (face & 1) + place) for face in send_faces
        ]
        out = jnp.where(first_half, outs[0], outs[1])
        for j in range(3):
            q = [out[min(4 * j + i, 9)] for i in range(4)]
            odd = (row & 1) == 1
            q = [
                jnp.where(odd, pltpu.roll(q[1], 1, 0), q[0]),
                jnp.where(odd, q[1], pltpu.roll(q[0], 7, 0)),
                jnp.where(odd, pltpu.roll(q[3], 1, 0), q[2]),
                jnp.where(odd, q[3], pltpu.roll(q[2], 7, 0)),
            ]
            upper = (row & 2) == 2
            q = [
                jnp.where(upper, pltpu.roll(q[2], 2, 0), q[0]),
                jnp.where(upper, pltpu.roll(q[3], 2, 0), q[1]),
                jnp.where(upper, q[2], pltpu.roll(q[0], 6, 0)),
                jnp.where(upper, q[3], pltpu.roll(q[1], 6, 0)),
            ]
            for r in range(4):
                tx_ref[turn, r, j] = q[r]
            v0, v1 = 2 * j, min(2 * j + 1, 4)
            tz_ref[turn, 0, j] = jnp.where(low_rows, turned[2 * v0 + 1], swapped[2 * v1 + 1])
            tz_ref[turn, 1, j] = jnp.where(low_rows, swapped[2 * v0], turned[2 * v1])

    def copies(turn):
        return [
            pltpu.make_async_remote_copy(
                src_ref=tx_ref.at[turn, i] if i < 4 else tz_ref.at[turn, i - 4],
                dst_ref=rx_ref.at[turn, i] if i < 4 else rz_ref.at[turn, i - 4],
                send_sem=tx_sem.at[turn, i],
                recv_sem=rx_sem.at[turn, i],
                device_id=peers[i],
                device_id_type=MESH,
            )
            for i in range(6)
        ]

    def volume(q, acc):
        sides = []
        for t in range(4):
            flat = q[t].reshape(80, 128)
            high = flat.astype(jnp.bfloat16)
            low = (flat - high.astype(jnp.float32)).astype(jnp.bfloat16)
            sides.append(jnp.concatenate([high, low, high], axis=1))
        plane = jnp.dot(
            jnp.concatenate(sides, axis=0), plane_ref[...], preferred_element_type=jnp.float32
        )
        rolled = [pltpu.roll(tile, 64, 2) for tile in q]
        for t in range(4):
            depth = None
            for s in range(4):
                for part_in, tile in ((0, q[s]), (1, rolled[s])):
                    at = (t * 4 + s) * 2 + part_in
                    term = depth_ref[at : at + 1, :] * tile
                    depth = term if depth is None else depth + term
            flat = plane[80 * t : 80 * t + 80]
            slopes = [
                flat[:, :128].reshape(5, 2, 8, 128),
                flat[:, 128:].reshape(5, 2, 8, 128),
                depth.reshape(5, 2, 8, 128),
            ]
            total = [
                along[0] * slopes[0][v] + along[1] * slopes[1][v] + along[2] * slopes[2][v]
                for v in range(5)
            ]
            for d in range(3):
                total[1 + d] = total[1 + d] + by_rho[d] * slopes[d][0] + by_stiff[d] * slopes[d][4]
                total[4] = total[4] + by_inverse[d] * slopes[d][1 + d]
            for v in range(5):
                acc[v, :, 128 * t : 128 * t + 128] = total[v].reshape(16, 128)

    def surface(d, difference):
        g = difference.reshape(5, 2, 8, 128)
        out = [face_all[d] * g[v] for v in range(5)]
        out[1 + d] = out[1 + d] + face_rho[d] * g[0] + face_stiff[d] * g[4]
        out[4] = out[4] + face_inverse[d] * g[1 + d]
        return jnp.stack(out, axis=0).reshape(10, 8, 128)

    def lifted(locals_in, pair_x, pair_y, pair_z, turned, turn):
        remote = []
        for r in range(4):
            boxes = [rx_ref[turn, r, j] for j in range(3)]
            remote.append(
                jnp.stack([rows(boxes[vh >> 2], group + (vh & 3)) for vh in range(10)], axis=0)
            )
        pieces = []
        for d, own in ((0, pair_x), (1, pair_y)):
            sides = []
            for f in (2 * d, 2 * d + 1):
                face = sources[f]
                chosen = locals_in[f]
                for r in range(4):
                    chosen = jnp.where((face >> 1) == 8 + r, remote[r], chosen)
                sides.append(lanes(chosen, 64 * (face & 1) + (place ^ (7 * flips[f]))))
            outer = jnp.where(first_half, sides[0], sides[1])
            tag = jnp.where(first_half, tags[2 * d], tags[2 * d + 1])
            plain = jnp.where(tag == 1, 0.0, -1.0)
            normal = jnp.where(tag == 1, -2.0, -1.0)
            own5, outer5 = own.reshape(5, 2, 8, 128), outer.reshape(5, 2, 8, 128)
            difference = jnp.stack(
                [
                    jnp.where(
                        tag == 0, outer5[v] - own5[v], (normal if v == 1 + d else plain) * own5[v]
                    )
                    for v in range(5)
                ],
                axis=0,
            )
            pieces.append(surface(d, difference))
        outers = []
        for v in range(5):
            below, above = rz_ref[turn, 0, v >> 1], rz_ref[turn, 1, v >> 1]
            if v & 1:
                below = pltpu.roll(below, 4, 0)
            else:
                above = pltpu.roll(above, 4, 0)
            t0, t1 = turned[2 * v], turned[2 * v + 1]
            inner = jnp.where(low_rows, t0, t1)
            outers.append(jnp.where(first_half, jnp.where(low_rows, below, t0), inner))
            outers.append(jnp.where(first_half, inner, jnp.where(low_rows, t1, above)))
        piece_z = surface(2, jnp.stack(outers, axis=0) - pair_z)
        result = []
        for t in range(4):
            total = jnp.where(on_x, lanes(pieces[0], to_x + 16 * t), 0.0) + jnp.where(
                on_y, lanes(pieces[1], to_y + 16 * t), 0.0
            )
            if t == 0:
                total = total + jnp.where(first_half, piece_z, 0.0)
            if t == 3:
                total = total + jnp.where(first_half, 0.0, piece_z)
            result.append(total)
        return result

    loads[0].wait()
    loads[1].wait()
    send_faces = []
    for k in range(2):
        face = jnp.zeros((8, 128), jnp.int32)
        for r in range(4):
            face = jnp.where(column == r, send_ref[k : k + 1, r : r + 1], face)
        send_faces.append(face)
    q = tiles_of(q_ref)
    pair_x, pair_y, pair_z = traces(q)
    swapped = pltpu.roll(pair_z, 64, 2)
    turned = pltpu.roll(swapped, 4, 1)
    send(pair_x, pair_y, swapped, turned, send_faces, 0)
    pl.semaphore_wait(barrier, 6)
    first = copies(0)
    for copy in first:
        copy.start()

    for load in loads[2:]:
        load.wait()
    sixteen = lax.broadcasted_iota(jnp.int32, (16, 16), 0) == lax.broadcasted_iota(jnp.int32, (16, 16), 1)

    def upright(line):
        spread = jnp.where(sixteen, jnp.broadcast_to(line, (16, 16)), 0.0)
        return jnp.broadcast_to(jnp.sum(spread, axis=1, keepdims=True), (16, 128)).reshape(2, 8, 128)

    rho, pressure = upright(rho_ref[...]), upright(pres_ref[...])
    stiff = gamma_gas * pressure
    inverse = 1.0 / rho
    sound = jnp.sqrt(stiff / rho)
    sign = jnp.where(first_half, -0.5 * lift_end, 0.5 * lift_end)
    along, by_rho, by_stiff, by_inverse = [], [], [], []
    face_all, face_rho, face_stiff, face_inverse = [], [], [], []
    for d in range(3):
        speed = upright(vel_ref[d : d + 1, :])
        scale = time_step * upright(met_ref[d : d + 1, :])
        along.append(scale * speed)
        by_rho.append(scale * rho)
        by_stiff.append(scale * stiff)
        by_inverse.append(scale * inverse)
        face_all.append(sign * along[d] + 0.5 * lift_end * scale * (jnp.abs(speed) + sound))
        face_rho.append(sign * by_rho[d])
        face_stiff.append(sign * by_stiff[d])
        face_inverse.append(sign * by_inverse[d])

    def spread_column(ref, f):
        one = jnp.broadcast_to(ref[:, f : f + 1], (4, 128))
        return jnp.concatenate([one, one], axis=0)

    sources = [spread_column(src_ref, f) for f in range(4)]
    flips = [spread_column(flip_ref, f) for f in range(4)]
    tags = [spread_column(tag_ref, f) for f in range(4)]

    locals_in = [picked(pair_x, pair_y, sources[f]) for f in range(4)]
    volume(q, acc_ref)
    for copy in first:
        copy.wait_recv()
    surf = lifted(locals_in, pair_x, pair_y, pair_z, turned, 0)
    middle = []
    for t in range(4):
        at = slice(128 * t, 128 * t + 128)
        section = acc_ref[:, :, at].reshape(10, 8, 128) + surf[t]
        middle.append(q_ref[:, :, at].reshape(10, 8, 128) + section_b1 * section)
        mid_ref[:, :, at] = middle[t].reshape(5, 16, 128)
        keep_ref[:, :, at] = (section_a2 * section).reshape(5, 16, 128)

    pair_x, pair_y, pair_z = traces(middle)
    swapped = pltpu.roll(pair_z, 64, 2)
    turned = pltpu.roll(swapped, 4, 1)
    send(pair_x, pair_y, swapped, turned, send_faces, 1)
    second = copies(1)
    for copy in second:
        copy.start()
    locals_in = [picked(pair_x, pair_y, sources[f]) for f in range(4)]
    volume(middle, acc_ref)
    for copy in second:
        copy.wait_recv()
    surf = lifted(locals_in, pair_x, pair_y, pair_z, turned, 1)
    for t in range(4):
        at = slice(128 * t, 128 * t + 128)
        register = (keep_ref[:, :, at] + acc_ref[:, :, at]).reshape(10, 8, 128) + surf[t]
        out_ref[1, :, :, at] = register.reshape(5, 16, 128)
        out_ref[0, :, :, at] = mid_ref[:, :, at] + section_b2 * register.reshape(5, 16, 128)
    stores = [
        pltpu.make_async_copy(out_ref.at[0], next_hbm, out_sem.at[0]),
        pltpu.make_async_copy(out_ref.at[1], reg_hbm, out_sem.at[1]),
    ]
    for store in stores:
        store.start()
    for copy in first + second:
        copy.wait_send()
    for store in stores:
        store.wait()


def on_device(
    adjoint, density, velocity, pressure, metric, face_source, face_flip, face_tag, send_list
):
    fields = jnp.transpose(adjoint, (1, 0, 2))
    state = pltpu.VMEM((5, 16, 512), jnp.float32)
    following, register = pl.pallas_call(
        kernel,
        out_shape=[jax.ShapeDtypeStruct((5, 16, 512), jnp.float32)] * 2,
        in_specs=[pl.BlockSpec(memory_space=pl.ANY)] * 11,
        out_specs=[pl.BlockSpec(memory_space=pl.ANY)] * 2,
        scratch_shapes=[
            state, state, state, state,
            pltpu.VMEM((2, 5, 16, 512), jnp.float32),
            pltpu.VMEM((1, 16), jnp.float32),
            pltpu.VMEM((3, 16), jnp.float32),
            pltpu.VMEM((1, 16), jnp.float32),
            pltpu.VMEM((3, 16), jnp.float32),
            pltpu.VMEM((4, 4), jnp.int32),
            pltpu.VMEM((4, 4), jnp.int32),
            pltpu.VMEM((4, 4), jnp.int32),
            pltpu.VMEM((2, 4), jnp.int32),
            pltpu.VMEM((384, 256), jnp.bfloat16),
            pltpu.VMEM((32, 128), jnp.float32),
            pltpu.VMEM((2, 4, 3, 8, 128), jnp.float32),
            pltpu.VMEM((2, 2, 3, 8, 128), jnp.float32),
            pltpu.VMEM((2, 4, 3, 8, 128), jnp.float32),
            pltpu.VMEM((2, 2, 3, 8, 128), jnp.float32),
            pltpu.SemaphoreType.DMA((11,)),
            pltpu.SemaphoreType.DMA((2,)),
            pltpu.SemaphoreType.DMA((2, 6)),
            pltpu.SemaphoreType.DMA((2, 6)),
        ],
        compiler_params=pltpu.CompilerParams(collective_id=0, has_side_effects=True),
        name="sections",
    )(
        fields,
        density.reshape(1, -1),
        velocity,
        pressure.reshape(1, -1),
        metric,
        face_source,
        face_flip,
        face_tag,
        jnp.transpose(send_list),
        jnp.asarray(plane_table()),
        jnp.asarray(depth_table()),
    )
    return jnp.transpose(following, (1, 0, 2)), jnp.transpose(register, (1, 0, 2))


def solution(mesh):
    placed = (
        P(("span", "elem"), None, None),
        P(("span", "elem")),
        P(None, ("span", "elem")),
        P(("span", "elem")),
        P(None, ("span", "elem")),
        P("elem", None),
        P("elem", None),
        P("elem", None),
        P("elem", None),
    )
    return jax.shard_map(
        on_device,
        mesh=mesh,
        in_specs=placed,
        out_specs=(P(("span", "elem"), None, None), P(("span", "elem"), None, None)),
        check_vma=False,
    )
```

time: 122 us -> 35.2 us (0.29)
  the two profiles are of different devices: /device:TPU:1 before, /device:TPU:8 now
where the time goes in v1:
time: 35.2 us; the launch traced here: 35 us
  Pallas kernels  32 us (91%)
  local copies, waits for them, and re-layouts  2.3 us (7%)
  between operations  0.65 us (2%)
    pallas_call x1, Pallas kernels, on_device(): pl.pallas_call(kernel, out_shape=[jax.ShapeDtypeStruct((5, 16, 512), jnp....  32 us
    unnamed x4, local copies, waits for them, and re-layouts  2.3 us

profile of v1, /device:TPU:8, one launch (start us, length us, event | category | flops | bytes accessed | tf_op | source)
XLA Modules:
  0.0 35.0 jit_solution(4910141747602721854)
XLA Ops:
  0.6 32.0 %sections.1 = (f32[5,16,512]{2,1,0:T(8,128)}, f32[5,16,512]{2,1,0:T(8,128)}) custom-call(f32[5,16,512]{2,1,0:T(8,128)} %bitcast.6, f32[1,16]{1,0:T(1,128)} %bitcast.10, f32[3,16]{1,0:T(4,128)} %vel_hbm.1, f32[1,16]{1,0:T(1,128)} %bitcast.11, f32[3,16]{1,0:T(4,128)} %met_hbm.1, s32[4,4]{1,0:T(4,128)} %src_hbm.1, s32[4,4]{1,0:T(4,128)} %flip_hbm.1, ...), custom_call_target="tpu_custom_call" | custom-call | tf_op jit(solution)/shard_map/sections/pallas_call | solution.py:386
  32.7 0.0 copy-start
  32.7 1.6 %copy.15 = f32[16,5,512]{2,0,1:T(8,128)} copy(f32[16,5,512]{2,0,1:T(8,128)} %bitcast.8) | data formatting | bytes 327680
  34.3 0.0 copy-done
  34.3 0.7 %copy.16 = f32[16,5,512]{2,0,1:T(8,128)} copy(f32[16,5,512]{2,0,1:T(8,128)S(1)} %bitcast.7) | data formatting | bytes 327680
Async XLA Ops:
  32.7 1.6 %copy-start = (f32[5,16,512]{2,1,0:T(8,128)S(1)}, f32[5,16,512]{2,1,0:T(8,128)}, u32[]{:S(2)}) copy-start(f32[5,16,512]{2,1,0:T(8,128)} %get-tuple-element.5) | copy-start | bytes 491524

commit v2 on v1

--- a/solution.py
+++ b/solution.py
@@ -90,11 +90,11 @@
 
 def kernel(
     adj_hbm, rho_hbm, vel_hbm, pres_hbm, met_hbm, src_hbm, flip_hbm, tag_hbm, send_hbm, plane_hbm, depth_hbm,
-    next_hbm, reg_hbm,
-    q_ref, mid_ref, keep_ref, acc_ref, out_ref,
+    next_ref, reg_ref,
+    q_ref, mid_ref, keep_ref, acc_ref,
     rho_ref, vel_ref, pres_ref, met_ref, src_ref, flip_ref, tag_ref, send_ref, plane_ref, depth_ref,
     tx_ref, tz_ref, rx_ref, rz_ref,
-    in_sem, out_sem, tx_sem, rx_sem,
+    in_sem, tx_sem, rx_sem,
 ):
     n_elem, n_span = lax.axis_size("elem"), lax.axis_size("span")
     part, slab = lax.axis_index("elem"), lax.axis_index("span")
@@ -364,16 +364,19 @@
     for t in range(4):
         at = slice(128 * t, 128 * t + 128)
         register = (keep_ref[:, :, at] + acc_ref[:, :, at]).reshape(10, 8, 128) + surf[t]
-        out_ref[1, :, :, at] = register.reshape(5, 16, 128)
-        out_ref[0, :, :, at] = mid_ref[:, :, at] + section_b2 * register.reshape(5, 16, 128)
+        reg_ref[:, :, at] = register.reshape(5, 16, 128)
+        next_ref[:, :, at] = mid_ref[:, :, at] + section_b2 * register.reshape(5, 16, 128)
+    for copy in first + second:
+        copy.wait_send()
+
+
+def write(next_in, reg_in, next_out, reg_out, sem):
     stores = [
-        pltpu.make_async_copy(out_ref.at[0], next_hbm, out_sem.at[0]),
-        pltpu.make_async_copy(out_ref.at[1], reg_hbm, out_sem.at[1]),
+        pltpu.make_async_copy(next_in, next_out, sem.at[0]),
+        pltpu.make_async_copy(reg_in, reg_out, sem.at[1]),
     ]
     for store in stores:
         store.start()
-    for copy in first + second:
-        copy.wait_send()
     for store in stores:
         store.wait()
 
@@ -383,14 +386,13 @@
 ):
     fields = jnp.transpose(adjoint, (1, 0, 2))
     state = pltpu.VMEM((5, 16, 512), jnp.float32)
-    following, register = pl.pallas_call(
+    results = pl.pallas_call(
         kernel,
-        out_shape=[jax.ShapeDtypeStruct((5, 16, 512), jnp.float32)] * 2,
-        in_specs=[pl.BlockSpec(memory_space=pl.ANY)] * 11,
-        out_specs=[pl.BlockSpec(memory_space=pl.ANY)] * 2,
+        out_shape=[pltpu.VMEM((5, 16, 512), jnp.float32)] * 2,
+        in_specs=[pl.BlockSpec(memory_space=pltpu.HBM)] * 11,
+        out_specs=[pl.BlockSpec(memory_space=pltpu.VMEM)] * 2,
         scratch_shapes=[
             state, state, state, state,
-            pltpu.VMEM((2, 5, 16, 512), jnp.float32),
             pltpu.VMEM((1, 16), jnp.float32),
             pltpu.VMEM((3, 16), jnp.float32),
             pltpu.VMEM((1, 16), jnp.float32),
@@ -406,25 +408,37 @@
             pltpu.VMEM((2, 4, 3, 8, 128), jnp.float32),
             pltpu.VMEM((2, 2, 3, 8, 128), jnp.float32),
             pltpu.SemaphoreType.DMA((11,)),
-            pltpu.SemaphoreType.DMA((2,)),
             pltpu.SemaphoreType.DMA((2, 6)),
             pltpu.SemaphoreType.DMA((2, 6)),
         ],
         compiler_params=pltpu.CompilerParams(collective_id=0, has_side_effects=True),
         name="sections",
     )(
-        fields,
-        density.reshape(1, -1),
-        velocity,
-        pressure.reshape(1, -1),
-        metric,
-        face_source,
-        face_flip,
-        face_tag,
-        jnp.transpose(send_list),
-        jnp.asarray(plane_table()),
-        jnp.asarray(depth_table()),
-    )
+        *(
+            pltpu.with_memory_space_constraint(array, pltpu.HBM)
+            for array in (
+                fields,
+                density.reshape(1, -1),
+                velocity,
+                pressure.reshape(1, -1),
+                metric,
+                face_source,
+                face_flip,
+                face_tag,
+                jnp.transpose(send_list),
+                jnp.asarray(plane_table()),
+                jnp.asarray(depth_table()),
+            )
+        )
+    )
+    following, register = pl.pallas_call(
+        write,
+        out_shape=[jax.ShapeDtypeStruct((5, 16, 512), jnp.float32)] * 2,
+        in_specs=[pl.BlockSpec(memory_space=pltpu.VMEM)] * 2,
+        out_specs=[pl.BlockSpec(memory_space=pltpu.HBM)] * 2,
+        scratch_shapes=[pltpu.SemaphoreType.DMA((2,))],
+        name="write",
+    )(*(pltpu.with_memory_space_constraint(array, pltpu.VMEM) for array in results))
     return jnp.transpose(following, (1, 0, 2)), jnp.transpose(register, (1, 0, 2))
 
 

time: 35.2 us -> 32.9 us (0.935)
  local copies, waits for them, and re-layouts: 2.3 us -> 0 us
    unnamed x4 -> x0, local copies, waits for them, and re-layouts: 2.3 us -> none
    pallas_call x1 -> x2, Pallas kernels: 32 us -> 32.1 us  [the longest x1 31.3 us: on_device(): pl.pallas_call(kernel, out_shape=[pltpu.VMEM((5, 16, 512), jnp.float32)]...]
where the time goes in v2:
time: 32.9 us; the launch traced here: 32.7 us
  Pallas kernels  32.1 us (98%)
  between operations  0.64 us (2%)
    pallas_call x1, Pallas kernels, on_device(): pl.pallas_call(kernel, out_shape=[pltpu.VMEM((5, 16, 512), jnp.float32)]...  31.3 us
    pallas_call x1, Pallas kernels, on_device(): pl.pallas_call(write, out_shape=[jax.ShapeDtypeStruct((5, 16, 512), jnp.f...  0.74 us

profile of v2, /device:TPU:8, one launch (start us, length us, event | category | flops | bytes accessed | tf_op | source)
XLA Modules:
  0.0 32.7 jit_solution(7872061846614545593)
XLA Ops:
  0.6 31.3 %sections.1 = (f32[5,16,512]{2,1,0:T(8,128)S(1)}, f32[5,16,512]{2,1,0:T(8,128)S(1)}) custom-call(f32[5,16,512]{2,1,0:T(8,128)} %bitcast.6, f32[1,16]{1,0:T(1,128)} %bitcast.8, f32[3,16]{1,0:T(4,128)} %vel_hbm.1, f32[1,16]{1,0:T(1,128)} %bitcast.9, f32[3,16]{1,0:T(4,128)} %met_hbm.1, s32[4,4]{1,0:T(4,128)} %src_hbm.1, s32[4,4]{1,0:T(4,128)} %flip_hbm.1, ...), custom_call_target="tpu_custom_call" | custom-call | tf_op jit(solution)/shard_map/sections/pallas_call | solution.py:389
  32.0 0.7 %write.1 = (f32[5,16,512]{2,1,0:T(8,128)}, f32[5,16,512]{2,1,0:T(8,128)}) custom-call(f32[5,16,512]{2,1,0:T(8,128)S(1)} %get-tuple-element.6.next_in, f32[5,16,512]{2,1,0:T(8,128)S(1)} %get-tuple-element.7.reg_in), custom_call_target="tpu_custom_call" | custom-call | tf_op jit(solution)/shard_map/write/pallas_call | solution.py:434

commit v3 on v2

--- a/solution.py
+++ b/solution.py
@@ -15,6 +15,7 @@
 section_b1 = 1432997174477.0 / 9575080441755.0
 section_b2 = 5161836677717.0 / 13612068292357.0
 offsets = (1, 2, -1, -2)
+line = 32
 MESH = pl.DeviceIdType.MESH
 
 
@@ -90,20 +91,44 @@
 
 def kernel(
     adj_hbm, rho_hbm, vel_hbm, pres_hbm, met_hbm, src_hbm, flip_hbm, tag_hbm, send_hbm, plane_hbm, depth_hbm,
-    next_ref, reg_ref,
-    q_ref, mid_ref, keep_ref, acc_ref,
+    mid_ref, base_ref, side_ref,
+    q_ref, keep_ref, acc_ref,
     rho_ref, vel_ref, pres_ref, met_ref, src_ref, flip_ref, tag_ref, send_ref, plane_ref, depth_ref,
     tx_ref, tz_ref, rx_ref, rz_ref,
-    in_sem, tx_sem, rx_sem,
+    in_sem, tx_sem, rx_sem, rz_sem, pass_sem, late_sem,
 ):
     n_elem, n_span = lax.axis_size("elem"), lax.axis_size("span")
     part, slab = lax.axis_index("elem"), lax.axis_index("span")
     peers = [{"elem": lax.rem(part + n_elem + o, n_elem)} for o in offsets]
     peers += [{"span": lax.rem(slab + n_span + o, n_span)} for o in (1, -1)]
+    spot = lax.rem(part, line)
+    begin, begin_next = spot == 0, spot == 1
+    end, end_before = spot == line - 1, spot == line - 2
+    ones = [x.astype(jnp.int32) for x in (begin, begin_next, end_before, end)]
+
+    def shifted(amount):
+        return {"elem": lax.rem(part + n_elem + amount, n_elem)}
 
     barrier = pltpu.get_barrier_semaphore()
-    for peer in peers:
+
+    def greet(peer):
         pl.semaphore_signal(barrier, inc=1, device_id=peer, device_id_type=MESH)
+
+    for i in (3, 2, 4, 5):
+        greet(peers[i])
+
+    @pl.when(jnp.logical_not(end))
+    def _():
+        greet(peers[0])
+
+        @pl.when(jnp.logical_not(end_before))
+        def _():
+            greet(peers[1])
+
+    @pl.when(begin)
+    def _():
+        for amount in (line - 1, line - 2, line, line + 1):
+            greet(shifted(amount))
 
     loads = [
         pltpu.make_async_copy(src, dst, in_sem.at[i])
@@ -127,11 +152,6 @@
     from_x = ((lane >> 3) & 1) * 64 + (lane & 7) * 8 + 7 * half
     from_y = ((lane >> 3) & 1) * 64 + 56 * half + (lane & 7)
     quarter = place >> 4
-    node_i, node_j, node_k = lane & 7, (lane >> 3) & 7, lane >> 6
-    to_x = 64 * (node_i >> 2) + 8 * node_k + node_j
-    to_y = 64 * (node_j >> 2) + 8 * node_k + node_i
-    on_x = (node_i == 0) | (node_i == 7)
-    on_y = (node_j == 0) | (node_j == 7)
 
     def tiles_of(ref):
         return [ref[:, :, 128 * t : 128 * t + 128].reshape(10, 8, 128) for t in range(4)]
@@ -147,21 +167,20 @@
         index = group + ((face >> 2) & 3)
         return jnp.where((face & 2) == 0, rows(pair_x, index), rows(pair_y, index))
 
-    def send(pair_x, pair_y, swapped, turned, send_faces, turn):
+    def send_sides(pair_x, pair_y, turn):
         outs = [
             lanes(picked(pair_x, pair_y, face), 64 * (face & 1) + place) for face in send_faces
         ]
         out = jnp.where(first_half, outs[0], outs[1])
-        for j in range(3):
-            q = [out[min(4 * j + i, 9)] for i in range(4)]
-            odd = (row & 1) == 1
+        odd, upper = (row & 1) == 1, (row & 2) == 2
+        for j in range(2):
+            q = [out[4 * j + i] for i in range(4)]
             q = [
                 jnp.where(odd, pltpu.roll(q[1], 1, 0), q[0]),
                 jnp.where(odd, q[1], pltpu.roll(q[0], 7, 0)),
                 jnp.where(odd, pltpu.roll(q[3], 1, 0), q[2]),
                 jnp.where(odd, q[3], pltpu.roll(q[2], 7, 0)),
             ]
-            upper = (row & 2) == 2
             q = [
                 jnp.where(upper, pltpu.roll(q[2], 2, 0), q[0]),
                 jnp.where(upper, pltpu.roll(q[3], 2, 0), q[1]),
@@ -169,23 +188,54 @@
                 jnp.where(upper, q[3], pltpu.roll(q[1], 6, 0)),
             ]
             for r in range(4):
-                tx_ref[turn, r, j] = q[r]
+                tx_ref[turn, r, 8 * j : 8 * j + 8] = q[r]
+        for r in range(4):
+            index = (row & 2) * 2 + r
+            tx_ref[turn, r, 16:24] = jnp.where(odd, rows(out[9], index), rows(out[8], index))
+
+    def send_ends(swapped, turned, turn):
+        for j in range(3):
             v0, v1 = 2 * j, min(2 * j + 1, 4)
-            tz_ref[turn, 0, j] = jnp.where(low_rows, turned[2 * v0 + 1], swapped[2 * v1 + 1])
-            tz_ref[turn, 1, j] = jnp.where(low_rows, swapped[2 * v0], turned[2 * v1])
+            tz_ref[turn, 0, 8 * j : 8 * j + 8] = jnp.where(
+                low_rows, turned[2 * v0 + 1], swapped[2 * v1 + 1]
+            )
+            tz_ref[turn, 1, 8 * j : 8 * j + 8] = jnp.where(
+                low_rows, swapped[2 * v0], turned[2 * v1]
+            )
 
     def copies(turn):
         return [
             pltpu.make_async_remote_copy(
-                src_ref=tx_ref.at[turn, i] if i < 4 else tz_ref.at[turn, i - 4],
-                dst_ref=rx_ref.at[turn, i] if i < 4 else rz_ref.at[turn, i - 4],
+                src_ref=tx_ref.at[turn, i, 0:20] if i < 4 else tz_ref.at[turn, i - 4, 0:20],
+                dst_ref=rx_ref.at[turn, i, 0:20] if i < 4 else rz_ref.at[turn, i - 4, 0:20],
                 send_sem=tx_sem.at[turn, i],
-                recv_sem=rx_sem.at[turn, i],
+                recv_sem=rx_sem.at[turn, i] if i < 4 else rz_sem.at[turn, i - 4],
                 device_id=peers[i],
                 device_id_type=MESH,
             )
             for i in range(6)
         ]
+
+    def redirected(i, box, target):
+        return pltpu.make_async_remote_copy(
+            src_ref=tx_ref.at[0, i, 0:20],
+            dst_ref=rx_ref.at[0, box, 0:20],
+            send_sem=tx_sem.at[0, i],
+            recv_sem=rx_sem.at[0, box],
+            device_id=target,
+            device_id_type=MESH,
+        )
+
+    def forwarded(k):
+        box, r, amount = ((4, 2, line - 1), (6, 3, line - 1), (5, 3, line - 2))[k]
+        return pltpu.make_async_remote_copy(
+            src_ref=rx_ref.at[0, box, 0:20],
+            dst_ref=rx_ref.at[0, r, 0:20],
+            send_sem=pass_sem.at[k],
+            recv_sem=rx_sem.at[0, r],
+            device_id=shifted(amount),
+            device_id_type=MESH,
+        )
 
     def volume(q, acc):
         sides = []
@@ -228,12 +278,18 @@
         out[4] = out[4] + face_inverse[d] * g[1 + d]
         return jnp.stack(out, axis=0).reshape(10, 8, 128)
 
-    def lifted(locals_in, pair_x, pair_y, pair_z, turned, turn):
+    def side_pieces(locals_in, pair_x, pair_y, turn):
         remote = []
         for r in range(4):
-            boxes = [rx_ref[turn, r, j] for j in range(3)]
+            boxes = [rx_ref[turn, r, 8 * j : 8 * j + 8] for j in range(3)]
             remote.append(
-                jnp.stack([rows(boxes[vh >> 2], group + (vh & 3)) for vh in range(10)], axis=0)
+                jnp.stack(
+                    [
+                        rows(boxes[vh >> 2], group + (vh & 3) if vh < 8 else (group >> 1) + vh - 8)
+                        for vh in range(10)
+                    ],
+                    axis=0,
+                )
             )
         pieces = []
         for d, own in ((0, pair_x), (1, pair_y)):
@@ -259,9 +315,13 @@
                 axis=0,
             )
             pieces.append(surface(d, difference))
+        return pieces
+
+    def end_piece(pair_z, turned, turn):
         outers = []
         for v in range(5):
-            below, above = rz_ref[turn, 0, v >> 1], rz_ref[turn, 1, v >> 1]
+            at = 8 * (v >> 1)
+            below, above = rz_ref[turn, 0, at : at + 8], rz_ref[turn, 1, at : at + 8]
             if v & 1:
                 below = pltpu.roll(below, 4, 0)
             else:
@@ -270,18 +330,13 @@
             inner = jnp.where(low_rows, t0, t1)
             outers.append(jnp.where(first_half, jnp.where(low_rows, below, t0), inner))
             outers.append(jnp.where(first_half, inner, jnp.where(low_rows, t1, above)))
-        piece_z = surface(2, jnp.stack(outers, axis=0) - pair_z)
-        result = []
-        for t in range(4):
-            total = jnp.where(on_x, lanes(pieces[0], to_x + 16 * t), 0.0) + jnp.where(
-                on_y, lanes(pieces[1], to_y + 16 * t), 0.0
-            )
-            if t == 0:
-                total = total + jnp.where(first_half, piece_z, 0.0)
-            if t == 3:
-                total = total + jnp.where(first_half, 0.0, piece_z)
-            result.append(total)
-        return result
+        return surface(2, jnp.stack(outers, axis=0) - pair_z)
+
+    def add_ends(piece_z, acc):
+        tiles = tiles_of(acc)
+        tiles[0] = tiles[0] + jnp.where(first_half, piece_z, 0.0)
+        tiles[3] = tiles[3] + jnp.where(first_half, 0.0, piece_z)
+        return tiles
 
     loads[0].wait()
     loads[1].wait()
@@ -293,13 +348,41 @@
         send_faces.append(face)
     q = tiles_of(q_ref)
     pair_x, pair_y, pair_z = traces(q)
+    send_sides(pair_x, pair_y, 0)
     swapped = pltpu.roll(pair_z, 64, 2)
     turned = pltpu.roll(swapped, 4, 1)
-    send(pair_x, pair_y, swapped, turned, send_faces, 0)
-    pl.semaphore_wait(barrier, 6)
+    send_ends(swapped, turned, 0)
+    pl.semaphore_wait(barrier, 6 - ones[0] + ones[2] + ones[3])
+
+    @pl.when(end)
+    def _():
+        pl.semaphore_signal(late_sem, inc=1, device_id=shifted(1 - line), device_id_type=MESH)
+
     first = copies(0)
-    for copy in first:
-        copy.start()
+    starts = [
+        first[0],
+        first[1],
+        redirected(2, 2 + 2 * ones[0], shifted(-1 - (line - 1) * ones[0])),
+        redirected(
+            3,
+            3 + 2 * ones[0] + 3 * ones[1],
+            shifted(-2 - (line - 2) * ones[0] - (line - 1) * ones[1]),
+        ),
+    ]
+    for i in (1, 3, 0, 2):
+        starts[i].start()
+    first[4].start()
+    first[5].start()
+
+    @pl.when(begin)
+    def _():
+        for box in (4, 5, 6):
+            pltpu.make_async_copy(
+                rx_ref.at[0, box, 0:20], rx_ref.at[0, box, 0:20], rx_sem.at[0, box]
+            ).wait()
+        pl.semaphore_wait(late_sem, 1)
+        for k in (2, 1, 0):
+            forwarded(k).start()
 
     for load in loads[2:]:
         load.wait()
@@ -338,45 +421,85 @@
 
     locals_in = [picked(pair_x, pair_y, sources[f]) for f in range(4)]
     volume(q, acc_ref)
-    for copy in first:
-        copy.wait_recv()
-    surf = lifted(locals_in, pair_x, pair_y, pair_z, turned, 0)
+    first[4].wait_recv()
+    first[5].wait_recv()
+    base = add_ends(end_piece(pair_z, turned, 0), acc_ref)
+    for t in range(4):
+        acc_ref[:, :, 128 * t : 128 * t + 128] = base[t].reshape(5, 16, 128)
+    ahead_x, ahead_y, ahead_z = traces([q[t] + section_b1 * base[t] for t in range(4)])
+    for i in (0, 2, 1, 3):
+        first[i].wait_recv()
+    piece_x, piece_y = side_pieces(locals_in, pair_x, pair_y, 0)
+    high, low = place >> 3, place & 7
+    low_end, high_end = (low == 0) | (low == 7), (high == 0) | (high == 7)
+    across = 64 * (low >> 2) + 8 * high + 7 * half
+    pair_x = ahead_x + section_b1 * (piece_x + jnp.where(low_end, lanes(piece_y, across), 0.0))
+    pair_y = ahead_y + section_b1 * (piece_y + jnp.where(low_end, lanes(piece_x, across), 0.0))
+    send_sides(pair_x, pair_y, 1)
+    second = copies(1)
+    for i in (1, 3, 0, 2):
+        second[i].start()
+    pair_z = ahead_z + section_b1 * (
+        jnp.where(low_end, lanes(piece_x, 64 * (low >> 2) + 56 * half + high), 0.0)
+        + jnp.where(high_end, lanes(piece_y, 64 * (high >> 2) + 56 * half + low), 0.0)
+    )
+    swapped = pltpu.roll(pair_z, 64, 2)
+    turned = pltpu.roll(swapped, 4, 1)
+    send_ends(swapped, turned, 1)
+    second[4].start()
+    second[5].start()
+
     middle = []
     for t in range(4):
         at = slice(128 * t, 128 * t + 128)
-        section = acc_ref[:, :, at].reshape(10, 8, 128) + surf[t]
+        section = acc_ref[:, :, at].reshape(10, 8, 128) + spread(piece_x, piece_y, t)
         middle.append(q_ref[:, :, at].reshape(10, 8, 128) + section_b1 * section)
         mid_ref[:, :, at] = middle[t].reshape(5, 16, 128)
         keep_ref[:, :, at] = (section_a2 * section).reshape(5, 16, 128)
-
-    pair_x, pair_y, pair_z = traces(middle)
-    swapped = pltpu.roll(pair_z, 64, 2)
-    turned = pltpu.roll(swapped, 4, 1)
-    send(pair_x, pair_y, swapped, turned, send_faces, 1)
-    second = copies(1)
-    for copy in second:
-        copy.start()
     locals_in = [picked(pair_x, pair_y, sources[f]) for f in range(4)]
     volume(middle, acc_ref)
-    for copy in second:
-        copy.wait_recv()
-    surf = lifted(locals_in, pair_x, pair_y, pair_z, turned, 1)
+    second[4].wait_recv()
+    second[5].wait_recv()
+    base = add_ends(end_piece(pair_z, turned, 1), acc_ref)
     for t in range(4):
         at = slice(128 * t, 128 * t + 128)
-        register = (keep_ref[:, :, at] + acc_ref[:, :, at]).reshape(10, 8, 128) + surf[t]
-        reg_ref[:, :, at] = register.reshape(5, 16, 128)
-        next_ref[:, :, at] = mid_ref[:, :, at] + section_b2 * register.reshape(5, 16, 128)
+        base_ref[:, :, at] = keep_ref[:, :, at] + base[t].reshape(5, 16, 128)
+    for i in (0, 2, 1, 3):
+        second[i].wait_recv()
+    piece_x, piece_y = side_pieces(locals_in, pair_x, pair_y, 1)
+    side_ref[0] = piece_x
+    side_ref[1] = piece_y
     for copy in first + second:
         copy.wait_send()
 
-
-def write(next_in, reg_in, next_out, reg_out, sem):
-    stores = [
-        pltpu.make_async_copy(next_in, next_out, sem.at[0]),
-        pltpu.make_async_copy(reg_in, reg_out, sem.at[1]),
-    ]
-    for store in stores:
-        store.start()
+    @pl.when(begin)
+    def _():
+        for k in range(3):
+            forwarded(k).wait_send()
+
+
+def spread(piece_x, piece_y, t):
+    lane = lax.broadcasted_iota(jnp.int32, (8, 128), 1)
+    node_i, node_j, node_k = lane & 7, (lane >> 3) & 7, lane >> 6
+    to_x = 64 * (node_i >> 2) + 8 * node_k + node_j + 16 * t
+    to_y = 64 * (node_j >> 2) + 8 * node_k + node_i + 16 * t
+    on_x = (node_i == 0) | (node_i == 7)
+    on_y = (node_j == 0) | (node_j == 7)
+    return jnp.where(on_x, lanes(piece_x, to_x), 0.0) + jnp.where(on_y, lanes(piece_y, to_y), 0.0)
+
+
+def finish(mid_in, base_in, side_in, next_hbm, reg_hbm, out_ref, sem):
+    stores = []
+    for v in range(5):
+        piece_x, piece_y = side_in[0, 2 * v : 2 * v + 2], side_in[1, 2 * v : 2 * v + 2]
+        for t in range(4):
+            at = slice(128 * t, 128 * t + 128)
+            register = base_in[v, :, at] + spread(piece_x, piece_y, t).reshape(16, 128)
+            out_ref[1, v, :, at] = register
+            out_ref[0, v, :, at] = mid_in[v, :, at] + section_b2 * register
+        for k, target in enumerate((next_hbm, reg_hbm)):
+            stores.append(pltpu.make_async_copy(out_ref.at[k, v], target.at[v], sem.at[k, v]))
+            stores[-1].start()
     for store in stores:
         store.wait()
 
@@ -388,11 +511,11 @@
     state = pltpu.VMEM((5, 16, 512), jnp.float32)
     results = pl.pallas_call(
         kernel,
-        out_shape=[pltpu.VMEM((5, 16, 512), jnp.float32)] * 2,
+        out_shape=[state, state, pltpu.VMEM((2, 10, 8, 128), jnp.float32)],
         in_specs=[pl.BlockSpec(memory_space=pltpu.HBM)] * 11,
-        out_specs=[pl.BlockSpec(memory_space=pltpu.VMEM)] * 2,
+        out_specs=[pl.BlockSpec(memory_space=pltpu.VMEM)] * 3,
         scratch_shapes=[
-            state, state, state, state,
+            state, state, state,
             pltpu.VMEM((1, 16), jnp.float32),
             pltpu.VMEM((3, 16), jnp.float32),
             pltpu.VMEM((1, 16), jnp.float32),
@@ -403,13 +526,16 @@
             pltpu.VMEM((2, 4), jnp.int32),
             pltpu.VMEM((384, 256), jnp.bfloat16),
             pltpu.VMEM((32, 128), jnp.float32),
-            pltpu.VMEM((2, 4, 3, 8, 128), jnp.float32),
-            pltpu.VMEM((2, 2, 3, 8, 128), jnp.float32),
-            pltpu.VMEM((2, 4, 3, 8, 128), jnp.float32),
-            pltpu.VMEM((2, 2, 3, 8, 128), jnp.float32),
+            pltpu.VMEM((2, 4, 24, 128), jnp.float32),
+            pltpu.VMEM((2, 2, 24, 128), jnp.float32),
+            pltpu.VMEM((2, 7, 24, 128), jnp.float32),
+            pltpu.VMEM((2, 2, 24, 128), jnp.float32),
             pltpu.SemaphoreType.DMA((11,)),
             pltpu.SemaphoreType.DMA((2, 6)),
-            pltpu.SemaphoreType.DMA((2, 6)),
+            pltpu.SemaphoreType.DMA((2, 7)),
+            pltpu.SemaphoreType.DMA((2, 2)),
+            pltpu.SemaphoreType.DMA((3,)),
+            pltpu.SemaphoreType.REGULAR,
         ],
         compiler_params=pltpu.CompilerParams(collective_id=0, has_side_effects=True),
         name="sections",
@@ -432,12 +558,15 @@
         )
     )
     following, register = pl.pallas_call(
-        write,
+        finish,
         out_shape=[jax.ShapeDtypeStruct((5, 16, 512), jnp.float32)] * 2,
-        in_specs=[pl.BlockSpec(memory_space=pltpu.VMEM)] * 2,
+        in_specs=[pl.BlockSpec(memory_space=pltpu.VMEM)] * 3,
         out_specs=[pl.BlockSpec(memory_space=pltpu.HBM)] * 2,
-        scratch_shapes=[pltpu.SemaphoreType.DMA((2,))],
-        name="write",
+        scratch_shapes=[
+            pltpu.VMEM((2, 5, 16, 512), jnp.float32),
+            pltpu.SemaphoreType.DMA((2, 5)),
+        ],
+        name="finish",
     )(*(pltpu.with_memory_space_constraint(array, pltpu.VMEM) for array in results))
     return jnp.transpose(following, (1, 0, 2)), jnp.transpose(register, (1, 0, 2))
 

time: 32.9 us -> 31.4 us (0.954)
  Pallas kernels: 32.1 us -> 30.5 us
    pallas_call x2, Pallas kernels: 32.1 us -> 30.5 us  [the longest x1 29.6 us: on_device(): pl.pallas_call(kernel, out_shape=[state, state, pltpu.VMEM((2, 10, 8, 128...]
where the time goes in v3:
time: 31.4 us; the launch traced here: 31.2 us
  Pallas kernels  30.5 us (97%)
  between operations  0.64 us (2%)
    pallas_call x1, Pallas kernels, on_device(): pl.pallas_call(kernel, out_shape=[state, state, pltpu.VMEM((2, 10, 8, 128...  29.6 us
    pallas_call x1, Pallas kernels, on_device(): pl.pallas_call(finish, out_shape=[jax.ShapeDtypeStruct((5, 16, 512), jnp....  0.99 us

profile of v3, /device:TPU:8, one launch (start us, length us, event | category | flops | bytes accessed | tf_op | source)
XLA Modules:
  0.0 31.2 jit_solution(1839459902421782234)
XLA Ops:
  0.6 29.6 %sections.1 = (f32[5,16,512]{2,1,0:T(8,128)S(1)}, f32[5,16,512]{2,1,0:T(8,128)S(1)}, f32[2,10,8,128]{3,2,1,0:T(8,128)S(1)}) custom-call(f32[5,16,512]{2,1,0:T(8,128)} %bitcast.6, f32[1,16]{1,0:T(1,128)} %bitcast.8, f32[3,16]{1,0:T(4,128)} %vel_hbm.1, f32[1,16]{1,0:T(1,128)} %bitcast.9, f32[3,16]{1,0:T(4,128)} %met_hbm.1, s32[4,4]{1,0:T(4,128)} %src_hbm.1, ...), custom_call_target="tpu_custom_call" | custom-call | tf_op jit(solution)/shard_map/sections/pallas_call | solution.py:512
  30.2 1.0 %finish.1 = (f32[5,16,512]{2,1,0:T(8,128)}, f32[5,16,512]{2,1,0:T(8,128)}) custom-call(f32[5,16,512]{2,1,0:T(8,128)S(1)} %get-tuple-element.7.mid_in, f32[5,16,512]{2,1,0:T(8,128)S(1)} %get-tuple-element.8.base_in, f32[2,10,8,128]{3,2,1,0:T(8,128)S(1)} %get-tuple-element.9.side_in), custom_call_target="tpu_custom_call" | custom-call | tf_op jit(solution)/shard_map/finish/pallas_call | solution.py:560

commit v4 on v3

--- a/solution.py
+++ b/solution.py
@@ -95,7 +95,7 @@
     q_ref, keep_ref, acc_ref,
     rho_ref, vel_ref, pres_ref, met_ref, src_ref, flip_ref, tag_ref, send_ref, plane_ref, depth_ref,
     tx_ref, tz_ref, rx_ref, rz_ref,
-    in_sem, tx_sem, rx_sem, rz_sem, pass_sem, late_sem,
+    in_sem, tx_sem, rx_sem, rz_sem, pass_sem, late_sem, two_sem, span_sem,
 ):
     n_elem, n_span = lax.axis_size("elem"), lax.axis_size("span")
     part, slab = lax.axis_index("elem"), lax.axis_index("span")
@@ -103,32 +103,42 @@
     peers += [{"span": lax.rem(slab + n_span + o, n_span)} for o in (1, -1)]
     spot = lax.rem(part, line)
     begin, begin_next = spot == 0, spot == 1
-    end, end_before = spot == line - 1, spot == line - 2
-    ones = [x.astype(jnp.int32) for x in (begin, begin_next, end_before, end)]
+    end, last_two, last_four = spot == line - 1, spot >= line - 2, spot >= line - 4
+    even = lax.rem(slab, 2) == 0
+    short = jnp.logical_and(last_two, even)
+    one_begin, one_next, one_last, one_short = (
+        x.astype(jnp.int32) for x in (begin, begin_next, last_two, short)
+    )
 
     def shifted(amount):
         return {"elem": lax.rem(part + n_elem + amount, n_elem)}
 
     barrier = pltpu.get_barrier_semaphore()
 
-    def greet(peer):
-        pl.semaphore_signal(barrier, inc=1, device_id=peer, device_id_type=MESH)
-
-    for i in (3, 2, 4, 5):
-        greet(peers[i])
+    def signal(semaphore, peer):
+        pl.semaphore_signal(semaphore, inc=1, device_id=peer, device_id_type=MESH)
+
+    signal(barrier, peers[2])
 
     @pl.when(jnp.logical_not(end))
     def _():
-        greet(peers[0])
-
-        @pl.when(jnp.logical_not(end_before))
-        def _():
-            greet(peers[1])
+        signal(barrier, peers[0])
+
+    signal(barrier, peers[3])
+
+    @pl.when(jnp.logical_not(last_four))
+    def _():
+        signal(barrier, peers[1])
+
+    @pl.when(jnp.logical_not(jnp.logical_and(last_two, jnp.logical_not(even))))
+    def _():
+        signal(barrier, peers[4])
+        signal(barrier, peers[5])
 
     @pl.when(begin)
     def _():
         for amount in (line - 1, line - 2, line, line + 1):
-            greet(shifted(amount))
+            signal(barrier, shifted(amount))
 
     loads = [
         pltpu.make_async_copy(src, dst, in_sem.at[i])
@@ -168,10 +178,13 @@
         return jnp.where((face & 2) == 0, rows(pair_x, index), rows(pair_y, index))
 
     def send_sides(pair_x, pair_y, turn):
-        outs = [
-            lanes(picked(pair_x, pair_y, face), 64 * (face & 1) + place) for face in send_faces
-        ]
-        out = jnp.where(first_half, outs[0], outs[1])
+        here, there = [picked(pair_x, pair_y, face) for face in send_faces]
+        wanted = jnp.where(first_half, send_faces[0], send_faces[1]) & 1
+        out = jnp.where(
+            wanted == half,
+            jnp.where(first_half, here, there),
+            pltpu.roll(jnp.where(first_half, there, here), 64, 2),
+        )
         odd, upper = (row & 1) == 1, (row & 2) == 2
         for j in range(2):
             q = [out[4 * j + i] for i in range(4)]
@@ -278,28 +291,32 @@
         out[4] = out[4] + face_inverse[d] * g[1 + d]
         return jnp.stack(out, axis=0).reshape(10, 8, 128)
 
-    def side_pieces(locals_in, pair_x, pair_y, turn):
-        remote = []
-        for r in range(4):
+    def side_pieces(locals_in, pair_x, pair_y, turn, arrivals, order):
+        chosen = list(locals_in)
+
+        def take(r):
             boxes = [rx_ref[turn, r, 8 * j : 8 * j + 8] for j in range(3)]
-            remote.append(
-                jnp.stack(
-                    [
-                        rows(boxes[vh >> 2], group + (vh & 3) if vh < 8 else (group >> 1) + vh - 8)
-                        for vh in range(10)
-                    ],
-                    axis=0,
-                )
+            remote = jnp.stack(
+                [
+                    rows(boxes[vh >> 2], group + (vh & 3) if vh < 8 else (group >> 1) + vh - 8)
+                    for vh in range(10)
+                ],
+                axis=0,
             )
+            for f in range(4):
+                chosen[f] = jnp.where((sources[f] >> 1) == 8 + r, remote, chosen[f])
+
+        for r in order[:3]:
+            arrivals[r].wait_recv()
+        for r in order[:3]:
+            take(r)
+        arrivals[order[3]].wait_recv()
+        take(order[3])
         pieces = []
         for d, own in ((0, pair_x), (1, pair_y)):
             sides = []
             for f in (2 * d, 2 * d + 1):
-                face = sources[f]
-                chosen = locals_in[f]
-                for r in range(4):
-                    chosen = jnp.where((face >> 1) == 8 + r, remote[r], chosen)
-                sides.append(lanes(chosen, 64 * (face & 1) + (place ^ (7 * flips[f]))))
+                sides.append(lanes(chosen[f], 64 * (sources[f] & 1) + (place ^ (7 * flips[f]))))
             outer = jnp.where(first_half, sides[0], sides[1])
             tag = jnp.where(first_half, tags[2 * d], tags[2 * d + 1])
             plain = jnp.where(tag == 1, 0.0, -1.0)
@@ -352,27 +369,41 @@
     swapped = pltpu.roll(pair_z, 64, 2)
     turned = pltpu.roll(swapped, 4, 1)
     send_ends(swapped, turned, 0)
-    pl.semaphore_wait(barrier, 6 - ones[0] + ones[2] + ones[3])
+    pl.semaphore_wait(barrier, 6 - one_begin - 2 * one_short)
 
     @pl.when(end)
     def _():
-        pl.semaphore_signal(late_sem, inc=1, device_id=shifted(1 - line), device_id_type=MESH)
+        signal(late_sem, shifted(1 - line))
+
+    @pl.when(jnp.logical_and(last_four, jnp.logical_not(last_two)))
+    def _():
+        signal(two_sem, peers[1])
+
+    @pl.when(jnp.logical_and(last_two, jnp.logical_not(even)))
+    def _():
+        signal(span_sem, peers[4])
+        signal(span_sem, peers[5])
 
     first = copies(0)
-    starts = [
-        first[0],
-        first[1],
-        redirected(2, 2 + 2 * ones[0], shifted(-1 - (line - 1) * ones[0])),
-        redirected(
-            3,
-            3 + 2 * ones[0] + 3 * ones[1],
-            shifted(-2 - (line - 2) * ones[0] - (line - 1) * ones[1]),
-        ),
-    ]
-    for i in (1, 3, 0, 2):
-        starts[i].start()
-    first[4].start()
-    first[5].start()
+    back_one = redirected(2, 2 + 2 * one_begin, shifted(-1 - (line - 1) * one_begin))
+    back_two = redirected(
+        3,
+        3 + 2 * one_begin + 3 * one_next,
+        shifted(-2 - (line - 2) * one_begin - (line - 1) * one_next),
+    )
+    first[1].start()
+
+    @pl.when(jnp.logical_not(last_two))
+    def _():
+        back_two.start()
+
+    first[0].start()
+    back_one.start()
+
+    @pl.when(jnp.logical_not(short))
+    def _():
+        first[4].start()
+        first[5].start()
 
     @pl.when(begin)
     def _():
@@ -421,15 +452,25 @@
 
     locals_in = [picked(pair_x, pair_y, sources[f]) for f in range(4)]
     volume(q, acc_ref)
+
+    @pl.when(short)
+    def _():
+        pl.semaphore_wait(span_sem, 2)
+        first[4].start()
+        first[5].start()
+
     first[4].wait_recv()
     first[5].wait_recv()
     base = add_ends(end_piece(pair_z, turned, 0), acc_ref)
     for t in range(4):
         acc_ref[:, :, 128 * t : 128 * t + 128] = base[t].reshape(5, 16, 128)
     ahead_x, ahead_y, ahead_z = traces([q[t] + section_b1 * base[t] for t in range(4)])
-    for i in (0, 2, 1, 3):
-        first[i].wait_recv()
-    piece_x, piece_y = side_pieces(locals_in, pair_x, pair_y, 0)
+    @pl.when(last_two)
+    def _():
+        pl.semaphore_wait(two_sem, 1)
+        back_two.start()
+
+    piece_x, piece_y = side_pieces(locals_in, pair_x, pair_y, 0, first, (0, 1, 2, 3))
     high, low = place >> 3, place & 7
     low_end, high_end = (low == 0) | (low == 7), (high == 0) | (high == 7)
     across = 64 * (low >> 2) + 8 * high + 7 * half
@@ -464,9 +505,7 @@
     for t in range(4):
         at = slice(128 * t, 128 * t + 128)
         base_ref[:, :, at] = keep_ref[:, :, at] + base[t].reshape(5, 16, 128)
-    for i in (0, 2, 1, 3):
-        second[i].wait_recv()
-    piece_x, piece_y = side_pieces(locals_in, pair_x, pair_y, 1)
+    piece_x, piece_y = side_pieces(locals_in, pair_x, pair_y, 1, second, (0, 2, 3, 1))
     side_ref[0] = piece_x
     side_ref[1] = piece_y
     for copy in first + second:
@@ -536,6 +575,8 @@
             pltpu.SemaphoreType.DMA((2, 2)),
             pltpu.SemaphoreType.DMA((3,)),
             pltpu.SemaphoreType.REGULAR,
+            pltpu.SemaphoreType.REGULAR,
+            pltpu.SemaphoreType.REGULAR,
         ],
         compiler_params=pltpu.CompilerParams(collective_id=0, has_side_effects=True),
         name="sections",

time: 31.4 us -> 31.1 us (level)
  no operation moved by 1% of the time
where the time goes in v4:
time: 31.1 us; the launch traced here: 30.9 us
  Pallas kernels  30.3 us (97%)
  between operations  0.64 us (2%)
    pallas_call x1, Pallas kernels, on_device(): pl.pallas_call(kernel, out_shape=[state, state, pltpu.VMEM((2, 10, 8, 128...  29.3 us
    pallas_call x1, Pallas kernels, on_device(): pl.pallas_call(finish, out_shape=[jax.ShapeDtypeStruct((5, 16, 512), jnp....  0.99 us

profile of v4, /device:TPU:8, one launch (start us, length us, event | category | flops | bytes accessed | tf_op | source)
XLA Modules:
  0.0 30.9 jit_solution(9410763818124284453)
XLA Ops:
  0.6 29.3 %sections.1 = (f32[5,16,512]{2,1,0:T(8,128)S(1)}, f32[5,16,512]{2,1,0:T(8,128)S(1)}, f32[2,10,8,128]{3,2,1,0:T(8,128)S(1)}) custom-call(f32[5,16,512]{2,1,0:T(8,128)} %bitcast.6, f32[1,16]{1,0:T(1,128)} %bitcast.8, f32[3,16]{1,0:T(4,128)} %vel_hbm.1, f32[1,16]{1,0:T(1,128)} %bitcast.9, f32[3,16]{1,0:T(4,128)} %met_hbm.1, s32[4,4]{1,0:T(4,128)} %src_hbm.1, ...), custom_call_target="tpu_custom_call" | custom-call | tf_op jit(solution)/shard_map/sections/pallas_call | solution.py:551
  29.9 1.0 %finish.1 = (f32[5,16,512]{2,1,0:T(8,128)}, f32[5,16,512]{2,1,0:T(8,128)}) custom-call(f32[5,16,512]{2,1,0:T(8,128)S(1)} %get-tuple-element.7.mid_in, f32[5,16,512]{2,1,0:T(8,128)S(1)} %get-tuple-element.8.base_in, f32[2,10,8,128]{3,2,1,0:T(8,128)S(1)} %get-tuple-element.9.side_in), custom_call_target="tpu_custom_call" | custom-call | tf_op jit(solution)/shard_map/finish/pallas_call | solution.py:601

commit v5 on v4

--- a/solution.py
+++ b/solution.py
@@ -355,6 +355,19 @@
         tiles[3] = tiles[3] + jnp.where(first_half, 0.0, piece_z)
         return tiles
 
+    @pl.when(last_two)
+    def _():
+        pl.semaphore_wait(barrier, 6 - 2 * one_short)
+
+    @pl.when(end)
+    def _():
+        signal(late_sem, shifted(1 - line))
+
+    @pl.when(jnp.logical_and(last_two, jnp.logical_not(even)))
+    def _():
+        signal(span_sem, peers[4])
+        signal(span_sem, peers[5])
+
     loads[0].wait()
     loads[1].wait()
     send_faces = []
@@ -369,20 +382,13 @@
     swapped = pltpu.roll(pair_z, 64, 2)
     turned = pltpu.roll(swapped, 4, 1)
     send_ends(swapped, turned, 0)
-    pl.semaphore_wait(barrier, 6 - one_begin - 2 * one_short)
-
-    @pl.when(end)
-    def _():
-        signal(late_sem, shifted(1 - line))
+    @pl.when(jnp.logical_not(last_two))
+    def _():
+        pl.semaphore_wait(barrier, 6 - one_begin)
 
     @pl.when(jnp.logical_and(last_four, jnp.logical_not(last_two)))
     def _():
         signal(two_sem, peers[1])
-
-    @pl.when(jnp.logical_and(last_two, jnp.logical_not(even)))
-    def _():
-        signal(span_sem, peers[4])
-        signal(span_sem, peers[5])
 
     first = copies(0)
     back_one = redirected(2, 2 + 2 * one_begin, shifted(-1 - (line - 1) * one_begin))

time: 31.1 us -> 30.9 us (level)
  no operation moved by 1% of the time
where the time goes in v5:
time: 30.9 us; the launch traced here: 30.8 us
  Pallas kernels  30.1 us (97%)
  between operations  0.64 us (2%)
    pallas_call x1, Pallas kernels, on_device(): pl.pallas_call(kernel, out_shape=[state, state, pltpu.VMEM((2, 10, 8, 128...  29.1 us
    pallas_call x1, Pallas kernels, on_device(): pl.pallas_call(finish, out_shape=[jax.ShapeDtypeStruct((5, 16, 512), jnp....  0.99 us

profile of v5, /device:TPU:8, one launch (start us, length us, event | category | flops | bytes accessed | tf_op | source)
XLA Modules:
  0.0 30.8 jit_solution(2251838331405136194)
XLA Ops:
  0.6 29.1 %sections.1 = (f32[5,16,512]{2,1,0:T(8,128)S(1)}, f32[5,16,512]{2,1,0:T(8,128)S(1)}, f32[2,10,8,128]{3,2,1,0:T(8,128)S(1)}) custom-call(f32[5,16,512]{2,1,0:T(8,128)} %bitcast.6, f32[1,16]{1,0:T(1,128)} %bitcast.8, f32[3,16]{1,0:T(4,128)} %vel_hbm.1, f32[1,16]{1,0:T(1,128)} %bitcast.9, f32[3,16]{1,0:T(4,128)} %met_hbm.1, s32[4,4]{1,0:T(4,128)} %src_hbm.1, ...), custom_call_target="tpu_custom_call" | custom-call | tf_op jit(solution)/shard_map/sections/pallas_call | solution.py:557
  29.8 1.0 %finish.1 = (f32[5,16,512]{2,1,0:T(8,128)}, f32[5,16,512]{2,1,0:T(8,128)}) custom-call(f32[5,16,512]{2,1,0:T(8,128)S(1)} %get-tuple-element.7.mid_in, f32[5,16,512]{2,1,0:T(8,128)S(1)} %get-tuple-element.8.base_in, f32[2,10,8,128]{3,2,1,0:T(8,128)S(1)} %get-tuple-element.9.side_in), custom_call_target="tpu_custom_call" | custom-call | tf_op jit(solution)/shard_map/finish/pallas_call | solution.py:607

commit v6 on v5

--- a/solution.py
+++ b/solution.py
@@ -99,8 +99,13 @@
 ):
     n_elem, n_span = lax.axis_size("elem"), lax.axis_size("span")
     part, slab = lax.axis_index("elem"), lax.axis_index("span")
-    peers = [{"elem": lax.rem(part + n_elem + o, n_elem)} for o in offsets]
-    peers += [{"span": lax.rem(slab + n_span + o, n_span)} for o in (1, -1)]
+
+    def moved(place_now, amount, size):
+        after = place_now + amount
+        return after - size * (after >= size).astype(jnp.int32) + size * (after < 0).astype(jnp.int32)
+
+    peers = [{"elem": moved(part, o, n_elem)} for o in offsets]
+    peers += [{"span": moved(slab, o, n_span)} for o in (1, -1)]
     spot = lax.rem(part, line)
     begin, begin_next = spot == 0, spot == 1
     end, last_two, last_four = spot == line - 1, spot >= line - 2, spot >= line - 4
@@ -111,7 +116,7 @@
     )
 
     def shifted(amount):
-        return {"elem": lax.rem(part + n_elem + amount, n_elem)}
+        return {"elem": moved(part, amount, n_elem)}
 
     barrier = pltpu.get_barrier_semaphore()
 
@@ -505,6 +510,14 @@
         keep_ref[:, :, at] = (section_a2 * section).reshape(5, 16, 128)
     locals_in = [picked(pair_x, pair_y, sources[f]) for f in range(4)]
     volume(middle, acc_ref)
+    for copy in first:
+        copy.wait_send()
+
+    @pl.when(begin)
+    def _():
+        for k in range(3):
+            forwarded(k).wait_send()
+
     second[4].wait_recv()
     second[5].wait_recv()
     base = add_ends(end_piece(pair_z, turned, 1), acc_ref)
@@ -514,13 +527,8 @@
     piece_x, piece_y = side_pieces(locals_in, pair_x, pair_y, 1, second, (0, 2, 3, 1))
     side_ref[0] = piece_x
     side_ref[1] = piece_y
-    for copy in first + second:
+    for copy in second:
         copy.wait_send()
-
-    @pl.when(begin)
-    def _():
-        for k in range(3):
-            forwarded(k).wait_send()
 
 
 def spread(piece_x, piece_y, t):
@@ -535,15 +543,19 @@
 
 def finish(mid_in, base_in, side_in, next_hbm, reg_hbm, out_ref, sem):
     stores = []
-    for v in range(5):
-        piece_x, piece_y = side_in[0, 2 * v : 2 * v + 2], side_in[1, 2 * v : 2 * v + 2]
+    for begin_v, end_v in ((0, 3), (3, 5)):
+        some = slice(begin_v, end_v)
+        piece_x, piece_y = (side_in[k, 2 * begin_v : 2 * end_v] for k in range(2))
         for t in range(4):
             at = slice(128 * t, 128 * t + 128)
-            register = base_in[v, :, at] + spread(piece_x, piece_y, t).reshape(16, 128)
-            out_ref[1, v, :, at] = register
-            out_ref[0, v, :, at] = mid_in[v, :, at] + section_b2 * register
+            added = spread(piece_x, piece_y, t).reshape(end_v - begin_v, 16, 128)
+            register = base_in[some, :, at] + added
+            out_ref[1, some, :, at] = register
+            out_ref[0, some, :, at] = mid_in[some, :, at] + section_b2 * register
         for k, target in enumerate((next_hbm, reg_hbm)):
-            stores.append(pltpu.make_async_copy(out_ref.at[k, v], target.at[v], sem.at[k, v]))
+            stores.append(
+                pltpu.make_async_copy(out_ref.at[k, some], target.at[some], sem.at[k, begin_v])
+            )
             stores[-1].start()
     for store in stores:
         store.wait()

time: 30.9 us -> 30.9 us (level)
  no operation moved by 1% of the time
where the time goes in v6:
time: 30.9 us; the launch traced here: 30.7 us
  Pallas kernels  30.1 us (97%)
  between operations  0.64 us (2%)
    pallas_call x1, Pallas kernels, on_device(): pl.pallas_call(kernel, out_shape=[state, state, pltpu.VMEM((2, 10, 8, 128...  29.1 us
    pallas_call x1, Pallas kernels, on_device(): pl.pallas_call(finish, out_shape=[jax.ShapeDtypeStruct((5, 16, 512), jnp....  0.96 us

profile of v6, /device:TPU:8, one launch (start us, length us, event | category | flops | bytes accessed | tf_op | source)
XLA Modules:
  0.0 30.7 jit_solution(799091467550664954)
XLA Ops:
  0.6 29.1 %sections.1 = (f32[5,16,512]{2,1,0:T(8,128)S(1)}, f32[5,16,512]{2,1,0:T(8,128)S(1)}, f32[2,10,8,128]{3,2,1,0:T(8,128)S(1)}) custom-call(f32[5,16,512]{2,1,0:T(8,128)} %bitcast.6, f32[1,16]{1,0:T(1,128)} %bitcast.8, f32[3,16]{1,0:T(4,128)} %vel_hbm.1, f32[1,16]{1,0:T(1,128)} %bitcast.9, f32[3,16]{1,0:T(4,128)} %met_hbm.1, s32[4,4]{1,0:T(4,128)} %src_hbm.1, ...), custom_call_target="tpu_custom_call" | custom-call | tf_op jit(solution)/shard_map/sections/pallas_call | solution.py:569
  29.8 1.0 %finish.1 = (f32[5,16,512]{2,1,0:T(8,128)}, f32[5,16,512]{2,1,0:T(8,128)}) custom-call(f32[5,16,512]{2,1,0:T(8,128)S(1)} %get-tuple-element.7.mid_in, f32[5,16,512]{2,1,0:T(8,128)S(1)} %get-tuple-element.8.base_in, f32[2,10,8,128]{3,2,1,0:T(8,128)S(1)} %get-tuple-element.9.side_in), custom_call_target="tpu_custom_call" | custom-call | tf_op jit(solution)/shard_map/finish/pallas_call | solution.py:619
